TPU v7x, 32 devices: a whole 2x2x4 slice. The times are simulated.
32 devices in a mesh: slab: 8 (over y, x, core), tile: 4 (over z).
Axes of the slice: x: 2, y: 2, z: 4, core: 2. Of those that a mesh axis runs over, the one named last changes fastest.
Arguments:
- particle_features: bfloat16 [6, 131072], P(None, ('slab', 'tile')), may hold values from -6 to 6
- destination: int32 [131072, 1], P(('slab', 'tile')), may hold values from 0 to 7; in each aligned block of 4096 rows (0 to 4095, 4096 to 8191, ...) at most 2048 rows name the same one
- cell_index: int32 [131072], P(('slab', 'tile')), may hold values from 0 to 16383
- offset_code: int32 [131072], P(('slab', 'tile')), may hold values from 0 to 262143
- live_count: int32 [32], P(('slab', 'tile')), may hold values from 2048 to 4096, as said below
- lift_weight: bfloat16 [3, 3, 64, 18], replicated, may hold values from -0.5 to 0.5
- fine_weight: bfloat16 [3, 3, 64, 192], replicated, may hold values from -0.15625 to 0.15625
- down_weight: bfloat16 [2, 2, 2, 256, 64], replicated, may hold values from -0.25 to 0.25
- coarse_weight: bfloat16 [3, 3, 256, 768], replicated, may hold values from -0.078125 to 0.078125
- up_weight: bfloat16 [2, 2, 2, 64, 256], replicated, may hold values from -0.375 to 0.375
- merge_weight: bfloat16 [3, 3, 64, 192], replicated, may hold values from -0.15625 to 0.15625
- head_weight: bfloat16 [3, 64], replicated, may hold values from -0.75 to 0.75
Outputs:
- displacement: float32 [3, 32, 32, 128], P(None, 'slab', 'tile')
Inputs may be any that keep to these rules, and one draw needn't show every extreme that they name: `destination`: among the rows of one device, at most 2048 name the same slab; some slab is named by exactly 2048 of them. `live_count`: some device has all 4096 rows live.
All inputs are finite; a program needn't handle non-finite values.
Results may differ from a plain program's by a relative error of at most 0.024.
Values may be sent and summed in bfloat16 or wider, within the bound.
A program may use at most 192 MiB of HBM per device.

v0:
```python
import jax
import jax.numpy as jnp
from jax import lax
from jax.sharding import PartitionSpec as P

NX = 128
YT = 8
CZ = 4


slope = 0.1


def shifted(block, axis, distance):
    devices = range(lax.axis_size(axis))
    route = [((i - distance) % len(devices), i) for i in devices]
    return lax.ppermute(block, axis, route)


def with_halo(block, sides, width):
    for axis, dim in sides:
        count = lax.axis_size(axis)
        forward = [(i, i + 1) for i in range(count - 1)]
        forward.append((count - 1, 0))
        backward = [(target, source) for source, target in forward]
        low = lax.ppermute(
            lax.slice_in_dim(block, block.shape[dim] - width, None, axis=dim), axis, forward
        )
        high = lax.ppermute(lax.slice_in_dim(block, 0, width, axis=dim), axis, backward)
        block = jnp.concatenate([low, block, high], axis=dim)
    return block


def act(values):
    return jnp.maximum(values, slope * values)


def conv_rim(padded, weight):
    stacked = jnp.concatenate([jnp.roll(padded, 1, 3), padded, jnp.roll(padded, -1, 3)], 0)
    out_z = padded.shape[1] - 2
    out_y = padded.shape[2] - 2
    total = jnp.zeros((weight.shape[2], out_z, out_y, padded.shape[3]), jnp.float32)
    for a in range(3):
        for b in range(3):
            total = total + jnp.einsum(
                "oi,izyx->ozyx",
                weight[a, b],
                stacked[:, a : a + out_z, b : b + out_y],
                preferred_element_type=jnp.float32,
            )
    return total


def pack_rows(particle_features, destination, cell_index, offset_code, live_count, slabs, capacity):
    rows = particle_features.shape[1]
    target_slab = destination[:, 0]
    live = jnp.arange(rows, dtype=jnp.int32) < live_count[0]
    masked = jnp.where(live[None, :], particle_features, jnp.zeros_like(particle_features))
    labels = jnp.arange(slabs, dtype=jnp.int32)
    onehot = (target_slab[:, None] == labels[None, :]).astype(jnp.int32)
    per_slab = jnp.sum(onehot, 0)
    starts = jnp.cumsum(per_slab) - per_slab
    order = jnp.argsort(target_slab, stable=True)
    sorted_slab = target_slab[order]
    sorted_hot = (sorted_slab[:, None] == labels[None, :]).astype(jnp.int32)
    slot = jnp.arange(rows, dtype=jnp.int32) - jnp.sum(sorted_hot * starts[None, :], 1)
    place = sorted_slab * capacity + slot
    feature_buffer = jnp.zeros(
        (particle_features.shape[0], slabs * capacity), particle_features.dtype
    )
    feature_buffer = feature_buffer.at[:, place].set(masked[:, order])
    integers = jnp.stack([cell_index[order], offset_code[order]], 0)
    integer_buffer = jnp.zeros((2, slabs * capacity), jnp.int32).at[:, place].set(integers)
    return (feature_buffer, integer_buffer)


def deposit_local(features, integers, total_y):
    cells = integers[0]
    codes = integers[1]
    values = features.astype(jnp.float32)
    plane_z = cells // (total_y * NX)
    row_y = cells // NX % total_y
    col_x = cells % NX
    frac_z = (codes // 4096 % 64).astype(jnp.float32) / 64.0
    frac_y = (codes // 64 % 64).astype(jnp.float32) / 64.0
    frac_x = (codes % 64).astype(jnp.float32) / 64.0
    field = jnp.zeros((features.shape[0], (CZ + 1) * total_y * NX), jnp.float32)
    for a in range(2):
        for b in range(2):
            for k in range(2):
                weight_z = frac_z if a else 1.0 - frac_z
                weight_y = frac_y if b else 1.0 - frac_y
                weight_x = frac_x if k else 1.0 - frac_x
                corner = weight_z * weight_y * weight_x
                target = (
                    (plane_z + a) * (total_y * NX) + (row_y + b) % total_y * NX + (col_x + k) % NX
                )
                field = field.at[:, target].add(values * corner[None, :])
    return field.reshape(features.shape[0], CZ + 1, total_y, NX)


def body(
    particle_features,
    destination,
    cell_index,
    offset_code,
    live_count,
    lift_weight,
    fine_weight,
    down_weight,
    coarse_weight,
    up_weight,
    merge_weight,
    head_weight,
):
    slabs = lax.axis_size("slab")
    total_y = YT * lax.axis_size("tile")
    rows = particle_features.shape[1]
    capacity = min(rows, 4 * rows // slabs)
    feature_buffer, integer_buffer = pack_rows(
        particle_features, destination, cell_index, offset_code, live_count, slabs, capacity
    )
    arrived, arrived_ints = (
        lax.all_to_all(feature_buffer, "slab", split_axis=1, concat_axis=1, tiled=True),
        lax.all_to_all(integer_buffer, "slab", split_axis=1, concat_axis=1, tiled=True),
    )
    field = deposit_local(arrived, arrived_ints, total_y)
    summed = lax.psum_scatter(
        field.astype(jnp.bfloat16), "tile", scatter_dimension=2, tiled=True
    ).astype(jnp.float32)
    spilled = shifted(summed[:, CZ], "slab", 1)
    grid = summed[:, :CZ].at[:, 0].add(spilled)
    grid = grid.astype(jnp.bfloat16)
    padded = with_halo(grid, (("slab", 1), ("tile", 2)), 2)
    first_padded = act(conv_rim(padded, lift_weight)).astype(jnp.bfloat16)
    second = act(conv_rim(first_padded, fine_weight)).astype(jnp.bfloat16)
    channels, planes, width_y, width_x = second.shape
    blocks = second.reshape(channels, planes // 2, 2, width_y // 2, 2, width_x // 2, 2)
    lowered = act(
        jnp.einsum("abkoc,czaybxk->ozyx", down_weight, blocks, preferred_element_type=jnp.float32)
    ).astype(jnp.bfloat16)
    lowered_padded = with_halo(lowered, (("slab", 1), ("tile", 2)), 1)
    coarse = act(conv_rim(lowered_padded, coarse_weight)).astype(jnp.bfloat16)
    raised = jnp.einsum(
        "abkoc,czyx->ozaybxk", up_weight, coarse, preferred_element_type=jnp.float32
    ).reshape(up_weight.shape[3], planes, width_y, width_x)
    joined = (second.astype(jnp.float32) + raised).astype(jnp.bfloat16)
    joined_padded = with_halo(joined, (("slab", 1), ("tile", 2)), 1)
    merged = act(conv_rim(joined_padded, merge_weight)).astype(jnp.bfloat16)
    return jnp.einsum("oc,czyx->ozyx", head_weight, merged, preferred_element_type=jnp.float32)


def solution(mesh):
    placed = (
        P(None, ("slab", "tile")),
        P(("slab", "tile"), None),
        P(("slab", "tile")),
        P(("slab", "tile")),
        P(("slab", "tile")),
        P(),
        P(),
        P(),
        P(),
        P(),
        P(),
        P(),
    )
    return jax.shard_map(
        body, mesh=mesh, in_specs=placed, out_specs=P(None, "slab", "tile", None), check_vma=False
    )
```

profile of v0, /device:TPU:0, one launch (start us, length us, event | category | flops | bytes accessed | tf_op | source)
XLA Modules:
  0.0 1280.2 jit_solution(11648301057517176931)
XLA Ops:
  7.5 6.5 sort.17
  14.0 23.0 %gather_fusion = s32[4096]{0:T(1024)S(1)} fusion(s32[4096]{0:T(1024)S(1)} %bitcast.395, s32[4096]{0:T(1024)S(1)} %fusion.234), kind=kCustom, calls=%fused_computation | custom fusion | bytes 49152 | tf_op jit(solution)/shard_map/gather | solution.py:64
  37.8 23.0 %gather_fusion.1 = s32[4096]{0:T(1024)S(1)} fusion(s32[4096]{0:T(1024)S(1)} %copy-done.2, s32[4096]{0:T(1024)S(1)} %fusion.234), kind=kCustom, calls=%fused_computation.1 | custom fusion | bytes 49152 | tf_op jit(solution)/shard_map/gather | solution.py:72
  60.8 23.0 %gather_fusion.2 = s32[4096]{0:T(1024)S(1)} fusion(s32[4096]{0:T(1024)S(1)} %copy-done.3, s32[4096]{0:T(1024)S(1)} %fusion.234), kind=kCustom, calls=%fused_computation.2 | custom fusion | bytes 49152 | tf_op jit(solution)/shard_map/gather | solution.py:72
  84.6 14.3 %scatter_custom_fusion = s32[2,16384]{0,1:T(8,128)} fusion(s32[4096]{0:T(1024)S(1)} %bitcast.417, s32[4096,2]{1,0:T(8,128)S(1)} %copy.86, s32[]{:T(128)} %constant.183.clone.1), kind=kCustom, calls=%fused_computation.16 | custom fusion | bytes 131076 | tf_op jit(solution)/shard_map/scatter | solution.py:73
  98.9 5.9 copy.87
  104.8 5.2 all-to-all-start
  111.2 25.9 %scatter_custom_fusion.1 = bf16[6,16384]{0,1:T(8,128)(2,1)} fusion(s32[4096]{0:T(1024)S(1)} %bitcast.418, bf16[]{:T(256)} %constant.197.clone.1, bf16[6,4096]{0,1:T(8,128)(2,1)S(1)} %copy.88, s32[4096]{0:T(1024)S(1)} %fusion.234), kind=kCustom, calls=%fused_computation.33 | custom fusion | bytes 196610 | tf_op jit(solution)/shard_map/scatter | solution.py:71
  137.1 4.5 copy.89
  141.6 4.2 all-to-all-start.1
  150.8 1.9 all-to-all-done.1
  153.5 2.4 fusion.141
  155.9 5.7 copy.90
  161.6 5.7 copy.91
  167.3 5.4 copy.92
  172.6 5.3 copy.93
  177.9 5.3 copy.94
  183.3 5.3 copy.95
  188.6 5.3 copy.96
  193.9 5.3 copy.97
  199.2 115.5 %scatter_custom_fusion.2 = f32[6,20480]{0,1:T(8,128)} fusion(s32[16384]{0:T(1024)} %bitcast.412, f32[16384,6]{1,0:T(8,128)} %copy.90, f32[]{:T(128)} %constant.182.clone.1), kind=kCustom, calls=%fused_computation.14 | custom fusion | flops 98304 | bytes 492032 | tf_op jit(solution)/shard_map/scatter-add | solution.py:98
  314.7 117.4 %scatter_fusion = f32[6,20480]{0,1:T(8,128)} fusion(f32[6,20480]{0,1:T(8,128)} %scatter_custom_fusion.2, s32[16384]{0:T(1024)S(1)} %bitcast.409, f32[16384,6]{1,0:T(8,128)} %copy.91), kind=kCustom, calls=%fused_computation.7 | custom fusion | flops 98304 | bytes 1245184 | tf_op jit(solution)/shard_map/scatter-add | solution.py:98
  432.1 117.4 %scatter_fusion.1 = f32[6,20480]{0,1:T(8,128)} fusion(f32[6,20480]{0,1:T(8,128)} %scatter_fusion, s32[16384]{0:T(1024)S(1)} %bitcast.408, f32[16384,6]{1,0:T(8,128)} %copy.92), kind=kCustom, calls=%fused_computation.8 | custom fusion | flops 98304 | bytes 1245184 | tf_op jit(solution)/shard_map/scatter-add | solution.py:98
  549.5 117.4 %scatter_fusion.2 = f32[6,20480]{0,1:T(8,128)} fusion(f32[6,20480]{0,1:T(8,128)} %scatter_fusion.1, s32[16384]{0:T(1024)S(1)} %bitcast.407, f32[16384,6]{1,0:T(8,128)} %copy.93), kind=kCustom, calls=%fused_computation.9 | custom fusion | flops 98304 | bytes 1245184 | tf_op jit(solution)/shard_map/scatter-add | solution.py:98
  666.8 117.4 %scatter_fusion.3 = f32[6,20480]{0,1:T(8,128)} fusion(f32[6,20480]{0,1:T(8,128)} %scatter_fusion.2, s32[16384]{0:T(1024)S(1)} %bitcast.406, f32[16384,6]{1,0:T(8,128)} %copy.94), kind=kCustom, calls=%fused_computation.10 | custom fusion | flops 98304 | bytes 1245184 | tf_op jit(solution)/shard_map/scatter-add | solution.py:98
  784.2 117.5 %scatter_fusion.4 = f32[6,20480]{0,1:T(8,128)} fusion(f32[6,20480]{0,1:T(8,128)} %scatter_fusion.3, s32[16384]{0:T(1024)S(1)} %bitcast.405, f32[16384,6]{1,0:T(8,128)} %copy.95), kind=kCustom, calls=%fused_computation.11 | custom fusion | flops 98304 | bytes 1245184 | tf_op jit(solution)/shard_map/scatter-add | solution.py:98
  901.7 117.3 %scatter_fusion.5 = f32[6,20480]{0,1:T(8,128)} fusion(f32[6,20480]{0,1:T(8,128)} %scatter_fusion.4, s32[16384]{0:T(1024)S(1)} %bitcast.404, f32[16384,6]{1,0:T(8,128)} %copy.96), kind=kCustom, calls=%fused_computation.12 | custom fusion | flops 98304 | bytes 1245184 | tf_op jit(solution)/shard_map/scatter-add | solution.py:98
  1019.0 117.3 %scatter_fusion.6 = f32[6,20480]{0,1:T(8,128)} fusion(f32[6,20480]{0,1:T(8,128)} %scatter_fusion.5, s32[16384]{0:T(1024)S(1)} %bitcast.403, f32[16384,6]{1,0:T(8,128)} %copy.97), kind=kCustom, calls=%fused_computation.13 | custom fusion | flops 98304 | bytes 1245184 | tf_op jit(solution)/shard_map/scatter-add | solution.py:98
  1136.3 6.0 copy.98
  1143.4 26.5 %reduce-scatter.4.cloned.1.call-done = bf16[8,3840]{1,0:T(8,128)(2,1)} async-done(((bf16[32,3840]{1,0:T(8,128)(2,1)}), bf16[8,3840]{1,0:T(8,128)(2,1)}) %reduce-scatter.4.cloned.1.call-update) | async-done | bytes 61456
  1171.0 4.2 collective-permute-done
  1175.3 2.6 collective-permute-start.2
  1179.7 3.8 collective-permute-start.4
  1183.5 1.9 collective-permute-done.3
  1192.2 1.8 maximum_maximum_fusion
  1199.1 2.6 collective-permute-start.6
  1201.7 4.0 collective-permute-done.5
  1205.8 4.1 collective-permute-start.8
  1209.9 3.6 collective-permute-done.7
  1214.1 2.8 fusion.5
  1226.6 4.8 convolution_bitcast_fusion
  1231.4 3.3 copy.102
  1238.5 2.9 collective-permute-done.10
  1241.4 2.3 collective-permute-done.9
  1243.8 3.2 collective-permute-start.11
  1247.9 2.4 collective-permute-done.11
  1253.0 2.4 maximum_maximum_fusion.1
  1266.6 4.9 fusion.122
  (132 shorter events, 54.5 us)
Async XLA Ops:
  6.5 1220.1 %copy-start = (bf16[2,2,2,64,256]{4,3,2,1,0:T(8,128)(2,1)S(1)}, bf16[2,2,2,64,256]{4,3,2,1,0:T(8,128)(2,1)}, u32[]{:S(2)}) copy-start(bf16[2,2,2,64,256]{4,3,2,1,0:T(8,128)(2,1)} %param.23) | copy-start | bytes 786436
  6.5 7.4 copy-start.1
  37.0 0.7 copy-start.2
  37.8 23.0 %copy-start.3 = (s32[4096]{0:T(1024)S(1)}, s32[4096]{0:T(1024)}, u32[]{:S(2)}) copy-start(s32[4096]{0:T(1024)} %param.17) | copy-start | bytes 49156
  98.9 11.7 copy-start.13
  104.8 36.9 %all-to-all-start = ((s32[2,8,2048]{2,0,1:T(2,128)}), s32[2,8,2048]{2,0,1:T(2,128)S(1)}, u32[]{:S(2)}, u32[]{:S(2)}) async-start(s32[2,8,2048]{2,0,1:T(2,128)} %copy.87), calls=%async_computation | async-start | bytes 262144 | tf_op jit(solution)/shard_map/all_to_all | solution.py:125
  141.6 11.1 all-to-all-start.1
  145.8 1024.1 %reduce-scatter.4.cloned.1.call-start = ((), (), s32[]{:S(2)}) async-start(), calls=%async_computation.3 | async-start | bytes 307200
  152.8 0.7 copy-start.5
  199.2 115.5 %copy-start.12 = (s32[16384,1]{0,1:T(1,128)S(1)}, s32[16384,1]{0,1:T(1,128)}, u32[]{:S(2)}) copy-start(s32[16384,1]{0,1:T(1,128)} %get-tuple-element.63) | copy-start | bytes 196612
  314.7 117.4 %copy-start.11 = (s32[16384,1]{0,1:T(1,128)S(1)}, s32[16384,1]{0,1:T(1,128)}, u32[]{:S(2)}) copy-start(s32[16384,1]{0,1:T(1,128)} %get-tuple-element.65) | copy-start | bytes 196612
  432.1 117.4 %copy-start.10 = (s32[16384,1]{0,1:T(1,128)S(1)}, s32[16384,1]{0,1:T(1,128)}, u32[]{:S(2)}) copy-start(s32[16384,1]{0,1:T(1,128)} %get-tuple-element.64) | copy-start | bytes 196612
  549.4 117.4 %copy-start.9 = (s32[16384,1]{0,1:T(1,128)S(1)}, s32[16384,1]{0,1:T(1,128)}, u32[]{:S(2)}) copy-start(s32[16384,1]{0,1:T(1,128)} %get-tuple-element.59) | copy-start | bytes 196612
  666.8 117.4 %copy-start.8 = (s32[16384,1]{0,1:T(1,128)S(1)}, s32[16384,1]{0,1:T(1,128)}, u32[]{:S(2)}) copy-start(s32[16384,1]{0,1:T(1,128)} %get-tuple-element.27) | copy-start | bytes 196612
  1142.4 43.9 %copy-start.14 = (bf16[3,3,64,18]{2,3,1,0:T(8,128)(2,1)S(1)}, bf16[3,3,64,18]{2,3,1,0:T(8,128)(2,1)}, u32[]{:S(2)}) copy-start(bf16[3,3,64,18]{2,3,1,0:T(8,128)(2,1)} %param.19) | copy-start | bytes 62212
  1170.9 4.3 collective-permute-start
  1175.3 4.3 collective-permute-start.1
  1175.3 4.2 collective-permute-start.2
  1179.6 5.8 collective-permute-start.3
  1179.7 5.7 collective-permute-start.4
  1192.2 1.9 copy-start.6
  1197.3 1.3 copy-start.16
  1199.0 6.7 collective-permute-start.5
  1199.1 6.6 collective-permute-start.6
  1205.7 7.8 collective-permute-start.7
  1205.8 7.7 collective-permute-start.8
  1214.1 2.9 copy-start.4
  1237.7 3.8 collective-permute-start.10
  1238.5 5.3 collective-permute-start.9
  1243.8 6.5 collective-permute-start.11
  1247.0 4.8 collective-permute-start.12
  1253.0 2.4 copy-start.7
  1263.8 2.8 copy-start.15
Sparse Core Ops, SparseCore 0:
  1143.6 26.3 reduce-scatter.3
where the time goes:
time: 1290 us; the launch traced here: 1280 us
  other arithmetic  962 us (75%)
  local copies, waits for them, and re-layouts  183 us (14%)
  waiting for transfers between devices  53 us (4%)
  matrix products  39.8 us (3%)
  starting transfers between devices  27.8 us (2%)
  between operations  15.1 us (1%)
    scatter-add x8, other arithmetic, deposit_local(): field = field.at[:, target].add(values * corner[None, :])  937 us
    gather x2, local copies, waits for them, and re-layouts, pack_rows(): integers = jnp.stack([cell_index[order], offset_code[order]], 0)  46.1 us
    mul x8, local copies, waits for them, and re-layouts, deposit_local(): field = field.at[:, target].add(values * corner[None, :])  43.3 us
    dot_general x34, matrix products, conv_rim(): jnp.einsum('oi,izyx->ozyx', weight[a, b], stacked[:, a:a + out_z, b:b + o...  29.8 us
    unnamed x2, waiting for transfers between devices  26.6 us
    scatter x1, local copies, waits for them, and re-layouts, pack_rows(): feature_buffer = feature_buffer.at[:, place].set(masked[:, order])  25.9 us
  transfers between devices with their start and end apart: 16, of which 11 were waited for; matrix products, arithmetic and copies ran while one was open for 3% of the time, Pallas kernels for 0%

commit v1 on v0

v1 whole, which is shorter than its diff:
```python
import functools

import jax
import jax.numpy as jnp
from jax import lax
from jax.experimental import pallas as pl
from jax.experimental.pallas import tpu as pltpu
from jax.sharding import PartitionSpec as P

NX = 128
YT = 8
CZ = 4


slope = 0.1


def with_halo(block, sides, width):
    for axis, dim in sides:
        count = lax.axis_size(axis)
        forward = [(i, i + 1) for i in range(count - 1)]
        forward.append((count - 1, 0))
        backward = [(target, source) for source, target in forward]
        low = lax.ppermute(
            lax.slice_in_dim(block, block.shape[dim] - width, None, axis=dim), axis, forward
        )
        high = lax.ppermute(lax.slice_in_dim(block, 0, width, axis=dim), axis, backward)
        block = jnp.concatenate([low, block, high], axis=dim)
    return block


def act(values):
    return jnp.maximum(values, slope * values)


def conv_rim(padded, weight):
    stacked = jnp.concatenate([jnp.roll(padded, 1, 3), padded, jnp.roll(padded, -1, 3)], 0)
    out_z = padded.shape[1] - 2
    out_y = padded.shape[2] - 2
    total = jnp.zeros((weight.shape[2], out_z, out_y, padded.shape[3]), jnp.float32)
    for a in range(3):
        for b in range(3):
            total = total + jnp.einsum(
                "oi,izyx->ozyx",
                weight[a, b],
                stacked[:, a : a + out_z, b : b + out_y],
                preferred_element_type=jnp.float32,
            )
    return total


GROUP = 4
CHUNK = 512


def deposit_kernel(slabs, tiles, feat_ref, dest_ref, cell_ref, code_ref, live_ref, out_ref, right, acc):
    group = pl.program_id(0)
    rows = feat_ref.shape[1]
    attrs = feat_ref.shape[0]
    ny = tiles * YT
    nz = slabs * CZ
    f32 = jnp.float32

    @pl.when(group == 0)
    def _():
        def build(j, carry):
            at = pl.ds(pl.multiple_of(j * CHUNK, CHUNK), CHUNK)
            cells = cell_ref[:, at]
            codes = code_ref[:, at]
            lane = lax.broadcasted_iota(jnp.int32, (1, CHUNK), 1) + j * CHUNK
            live = lane < live_ref[0]
            feats = jnp.where(live, feat_ref[:, at].astype(f32), 0.0)
            frac = (codes & 63).astype(f32) * (1.0 / 64.0)
            col = cells & (NX - 1)
            nxt = (col + 1) & (NX - 1)
            xs = lax.broadcasted_iota(jnp.int32, (NX, CHUNK), 0)
            wx = jnp.where(xs == col, 1.0 - frac, 0.0) + jnp.where(xs == nxt, frac, 0.0)
            for c in range(attrs):
                right[c * NX : (c + 1) * NX, at] = (wx * feats[c : c + 1, :]).astype(jnp.bfloat16)
            return carry

        lax.fori_loop(0, rows // CHUNK, build, 0)

    def step(j, carry):
        at = pl.ds(pl.multiple_of(j * CHUNK, CHUNK), CHUNK)
        cells = cell_ref[:, at]
        codes = code_ref[:, at]
        fz = ((codes >> 12) & 63).astype(f32) * (1.0 / 64.0)
        fy = ((codes >> 6) & 63).astype(f32) * (1.0 / 64.0)
        row = cells // NX
        y0 = row % ny
        z0 = dest_ref[:, at] * CZ + row // ny
        y1 = (y0 + 1) % ny
        z1 = (z0 + 1) % nz
        ys = lax.broadcasted_iota(jnp.int32, (ny, CHUNK), 0)
        wy = jnp.where(ys == y0, 1.0 - fy, 0.0) + jnp.where(ys == y1, fy, 0.0)
        zs = lax.broadcasted_iota(jnp.int32, (GROUP * CZ, CHUNK), 0) + group * GROUP * CZ
        wz = jnp.where(zs == z0, 1.0 - fz, 0.0) + jnp.where(zs == z1, fz, 0.0)
        pieces = []
        for s in range(GROUP):
            for t in range(tiles):
                for z in range(CZ):
                    k = s * CZ + z
                    pieces.append(wz[k : k + 1, :] * wy[t * YT : (t + 1) * YT, :])
        left = jnp.concatenate(pieces, 0).astype(jnp.bfloat16)
        part = lax.dot_general(
            left, right[:, at], (((1,), (1,)), ((), ())), preferred_element_type=f32
        )

        @pl.when(j == 0)
        def _():
            acc[...] = part

        @pl.when(j > 0)
        def _():
            acc[...] += part

        return carry

    lax.fori_loop(0, rows // CHUNK, step, 0)
    size = CZ * YT
    for s in range(GROUP):
        for t in range(tiles):
            k = (s * tiles + t) * size
            for c in range(attrs):
                out_ref[s, t, c] = acc[k : k + size, c * NX : (c + 1) * NX].astype(jnp.bfloat16)


def deposit(features, destination, cell_index, offset_code, live_count, slabs, tiles):
    attrs, rows = features.shape
    size = CZ * YT
    whole = lambda shape: pl.BlockSpec(shape, lambda g: (0, 0))
    return pl.pallas_call(
        functools.partial(deposit_kernel, slabs, tiles),
        grid=(slabs // GROUP,),
        in_specs=[
            whole((attrs, rows)),
            whole((1, rows)),
            whole((1, rows)),
            whole((1, rows)),
            pl.BlockSpec(memory_space=pltpu.SMEM),
        ],
        out_specs=pl.BlockSpec((GROUP, tiles, attrs, size, NX), lambda g: (g, 0, 0, 0, 0)),
        out_shape=jax.ShapeDtypeStruct((slabs, tiles, attrs, size, NX), jnp.bfloat16),
        scratch_shapes=[
            pltpu.VMEM((attrs * NX, rows), jnp.bfloat16),
            pltpu.VMEM((GROUP * tiles * size, attrs * NX), jnp.float32),
        ],
        compiler_params=pltpu.CompilerParams(vmem_limit_bytes=48 << 20),
        name="deposit",
    )(
        features,
        destination.reshape(1, rows),
        cell_index.reshape(1, rows),
        offset_code.reshape(1, rows),
        live_count,
    )


def body(
    particle_features,
    destination,
    cell_index,
    offset_code,
    live_count,
    lift_weight,
    fine_weight,
    down_weight,
    coarse_weight,
    up_weight,
    merge_weight,
    head_weight,
):
    slabs = lax.axis_size("slab")
    tiles = lax.axis_size("tile")
    field = deposit(
        particle_features, destination, cell_index, offset_code, live_count, slabs, tiles
    )
    field = lax.all_to_all(field, "slab", split_axis=0, concat_axis=0, tiled=True)
    field = jnp.sum(field.astype(jnp.float32), 0).astype(jnp.bfloat16)
    field = lax.all_to_all(field, "tile", split_axis=0, concat_axis=0, tiled=True)
    grid = jnp.sum(field.astype(jnp.float32), 0).astype(jnp.bfloat16)
    grid = grid.reshape(grid.shape[0], CZ, YT, NX)
    padded = with_halo(grid, (("slab", 1), ("tile", 2)), 2)
    first_padded = act(conv_rim(padded, lift_weight)).astype(jnp.bfloat16)
    second = act(conv_rim(first_padded, fine_weight)).astype(jnp.bfloat16)
    channels, planes, width_y, width_x = second.shape
    blocks = second.reshape(channels, planes // 2, 2, width_y // 2, 2, width_x // 2, 2)
    lowered = act(
        jnp.einsum("abkoc,czaybxk->ozyx", down_weight, blocks, preferred_element_type=jnp.float32)
    ).astype(jnp.bfloat16)
    lowered_padded = with_halo(lowered, (("slab", 1), ("tile", 2)), 1)
    coarse = act(conv_rim(lowered_padded, coarse_weight)).astype(jnp.bfloat16)
    raised = jnp.einsum(
        "abkoc,czyx->ozaybxk", up_weight, coarse, preferred_element_type=jnp.float32
    ).reshape(up_weight.shape[3], planes, width_y, width_x)
    joined = (second.astype(jnp.float32) + raised).astype(jnp.bfloat16)
    joined_padded = with_halo(joined, (("slab", 1), ("tile", 2)), 1)
    merged = act(conv_rim(joined_padded, merge_weight)).astype(jnp.bfloat16)
    return jnp.einsum("oc,czyx->ozyx", head_weight, merged, preferred_element_type=jnp.float32)


def solution(mesh):
    placed = (
        P(None, ("slab", "tile")),
        P(("slab", "tile"), None),
        P(("slab", "tile")),
        P(("slab", "tile")),
        P(("slab", "tile")),
        P(),
        P(),
        P(),
        P(),
        P(),
        P(),
        P(),
    )
    return jax.shard_map(
        body, mesh=mesh, in_specs=placed, out_specs=P(None, "slab", "tile", None), check_vma=False
    )
```

time: 1290 us -> 154 us (0.12)
  other arithmetic: 962 us -> 9.73 us
  local copies, waits for them, and re-layouts: 183 us -> 12.4 us
  blocking collectives: 0 us -> 37.6 us
  waiting for transfers between devices: 53 us -> 18.9 us
  between operations: 15.1 us -> 1.12 us
  Pallas kernels: 0 us -> 13.6 us
    scatter-add x9 -> x0, other arithmetic: 937 us -> none  [the longest x8 937 us: deposit_local(): field = field.at[:, target].add(values * corner[None, :])]
    gather x3 -> x0, local copies, waits for them, and re-layouts: 69.1 us -> none  [the longest x2 46.1 us: pack_rows(): integers = jnp.stack([cell_index[order], offset_code[order]], 0)]
    mul x8 -> x0, local copies, waits for them, and re-layouts: 43.3 us -> none  [deposit_local(): field = field.at[:, target].add(values * corner[None, :])]
    scatter x2 -> x0, local copies, waits for them, and re-layouts: 40.2 us -> none  [the longest x1 25.9 us: pack_rows(): feature_buffer = feature_buffer.at[:, place].set(masked[:, order])]
    all_to_all x0 -> x2, blocking collectives: none -> 37.6 us  [the longest x1 25.9 us: body(): lax.all_to_all(field, 'slab', split_axis=0, concat_axis=0, tiled=True)]
    unnamed x2 -> x0, waiting for transfers between devices: 26.6 us -> none
    pallas_call x0 -> x1, Pallas kernels: none -> 13.6 us  [deposit(): pl.pallas_call(functools.partial(deposit_kernel, slabs, tiles), grid=(sla...]
  transfers between devices with their start and end apart: 16 -> 12, of which waited for: 11 -> 7; matrix products, arithmetic and copies ran while one was open for 3% -> 0% of each run, Pallas kernels for 0% -> 0%
where the time goes in v1:
time: 154 us; the launch traced here: 153 us
  matrix products  39.8 us (26%)
  blocking collectives  37.6 us (24%)
  starting transfers between devices  19.9 us (13%)
  waiting for transfers between devices  18.9 us (12%)
  Pallas kernels  13.6 us (9%)
  local copies, waits for them, and re-layouts  12.4 us (8%)
  other arithmetic  9.73 us (6%)
    dot_general x34, matrix products, conv_rim(): jnp.einsum('oi,izyx->ozyx', weight[a, b], stacked[:, a:a + out_z, b:b + o...  29.8 us
    all_to_all x1, blocking collectives, body(): lax.all_to_all(field, 'slab', split_axis=0, concat_axis=0, tiled=True)  25.9 us
    ppermute x6, waiting for transfers between devices, with_halo(): lax.ppermute(lax.slice_in_dim(block, block.shape[dim] - width, None, axis...  17 us
    ppermute x6, starting transfers between devices, with_halo(): lax.ppermute(lax.slice_in_dim(block, 0, width, axis=dim), axis, backward)  15.2 us
    pallas_call x1, Pallas kernels, deposit(): pl.pallas_call(functools.partial(deposit_kernel, slabs, tiles), grid=(sla...  13.6 us
    all_to_all x1, blocking collectives, body(): lax.all_to_all(field, 'tile', split_axis=0, concat_axis=0, tiled=True)  11.6 us
    concatenate x4, other arithmetic, conv_rim(): jnp.concatenate([jnp.roll(padded, 1, 3), padded, jnp.roll(padded, -1, 3)]...  7.64 us
    dot_general x1, matrix products, body(): jnp.einsum('oc,czyx->ozyx', head_weight, merged, preferred_element_type=j...  4.89 us
  transfers between devices with their start and end apart: 12, of which 7 were waited for; matrix products, arithmetic and copies ran while one was open for 0% of the time, Pallas kernels for 0%

profile of v1, /device:TPU:0, one launch (start us, length us, event | category | flops | bytes accessed | tf_op | source)
XLA Modules:
  0.0 153.1 jit_solution(2333357107211593865)
XLA Ops:
  0.7 0.8 copy-done.1
  1.5 0.7 copy-done.2
  2.3 0.7 copy-done.3
  3.0 0.7 copy-done.4
  3.7 13.6 %deposit.1 = bf16[8,4,6,32,128]{4,3,2,1,0:T(8,128)(2,1)S(1)} custom-call(bf16[6,4096]{1,0:T(8,128)(2,1)S(1)} %copy-done.1, s32[1,4096]{1,0:T(1,128)S(1)} %bitcast.341, s32[1,4096]{1,0:T(1,128)S(1)} %bitcast.342, s32[1,4096]{1,0:T(1,128)S(1)} %bitcast.343, s32[1]{0:T(128)S(6)} %copy.74.live_ref), custom_call_target="tpu_custom_call" | custom-call | tf_op jit(solution)/shard_map/deposit/pallas_call | solution.py:133
  17.3 25.9 %all_to_all.10 = bf16[8,4,6,32,128]{4,3,2,1,0:T(8,128)(2,1)S(1)} all-to-all(bf16[8,4,6,32,128]{4,3,2,1,0:T(8,128)(2,1)S(1)} %deposit.1), channel_id=1, replica_groups=mesh['slab'=8,'tile'=4] {'slab'}, dimensions={0} | all-to-all | bytes 3145728 | tf_op jit(solution)/shard_map/all_to_all | solution.py:179
  43.5 11.6 %all_to_all.11 = bf16[4,6,32,128]{3,2,1,0:T(8,128)(2,1)S(1)} all-to-all(bf16[4,6,32,128]{3,2,1,0:T(8,128)(2,1)S(1)} %reduce_sum.24), channel_id=1, replica_groups=mesh['slab'=8,'tile'=4] {'tile'}, dimensions={0} | all-to-all | bytes 393216 | tf_op jit(solution)/shard_map/all_to_all | solution.py:181
  55.3 2.6 %collective-permute-start.1 = (bf16[6,2,8,128]{3,0,2,1:T(8,128)(2,1)S(1)}, bf16[6,2,8,128]{3,0,2,1:T(8,128)(2,1)S(1)}, u32[]{:S(2)}, u32[]{:S(2)}) collective-permute-start(bf16[6,2,8,128]{3,0,2,1:T(8,128)(2,1)S(1)} %get-tuple-element.30), channel_id=1, source_target_pairs={{4,0},{8,4},{12,8},{16,12},{20,16},{24,20},{28,24},{0,28},{5,1},{9... | collective-permute-start | bytes 73736 | tf_op jit(solution)/shard_map/ppermute | solution.py:27
  57.9 1.6 %collective-permute-done = bf16[6,2,8,128]{3,0,2,1:T(8,128)(2,1)S(1)} collective-permute-done((bf16[6,2,8,128]{3,0,2,1:T(8,128)(2,1)S(1)}, bf16[6,2,8,128]{3,0,2,1:T(8,128)(2,1)S(1)}, u32[]{:S(2)}, u32[]{:S(2)}) %collective-permute-start) | collective-permute-done | bytes 24608 | tf_op jit(solution)/shard_map/ppermute | solution.py:24
  59.5 1.2 collective-permute-start.2
  60.7 2.7 %collective-permute-start.3 = (bf16[6,8,2,128]{3,0,2,1:T(8,128)(2,1)S(1)}, bf16[6,8,2,128]{3,0,2,1:T(8,128)(2,1)S(1)}, u32[]{:S(2)}, u32[]{:S(2)}) collective-permute-start(bf16[6,8,2,128]{3,0,2,1:T(8,128)(2,1)S(1)} %get-tuple-element.28), channel_id=1, source_target_pairs={{1,0},{2,1},{3,2},{0,3},{5,4},{6,5},{7,6},{4,7},{9,8},{10,9},{11,1... | collective-permute-start | bytes 73736 | tf_op jit(solution)/shard_map/ppermute | solution.py:27
  63.4 2.1 %collective-permute-done.2 = bf16[6,8,2,128]{3,0,2,1:T(8,128)(2,1)S(1)} collective-permute-done((bf16[6,8,2,128]{3,0,2,1:T(8,128)(2,1)S(1)}, bf16[6,8,2,128]{3,0,2,1:T(8,128)(2,1)S(1)}, u32[]{:S(2)}, u32[]{:S(2)}) %collective-permute-start.2) | collective-permute-done | bytes 24608 | tf_op jit(solution)/shard_map/ppermute | solution.py:24
  70.1 1.2 fusion.4
  72.3 1.8 %maximum_maximum_fusion = bf16[192,6,10,128]{3,0,2,1:T(8,128)(2,1)S(1)} fusion(bf16[64,6,10,1]{3,0,2,1:T(8,128)(2,1)S(1)} %get-tuple-element.10, bf16[64,6,10,127]{3,0,2,1:T(8,128)(2,1)S(1)} %get-tuple-element.12, bf16[64,6,10,128]{3,0,2,1:T(8,128)(2,1)S(1)} %fusion.4, bf16[64,6,10,127]{3,0,2,1:T(8,128)(2,1)S(1)} %get-tuple-element.11, ...), kind=kLoop, calls=%fused_computation | loop fusion | flops 14745600 | bytes 5898240 | tf_op jit(solution)/shard_map/concatenate | solution.py:37
  77.5 0.8 fusion.99
  79.4 2.6 %collective-permute-start.5 = (bf16[256,1,4,64]{0,3,2,1:T(8,128)(2,1)S(1)}, bf16[256,1,4,64]{0,3,2,1:T(8,128)(2,1)S(1)}, u32[]{:S(2)}, u32[]{:S(2)}) collective-permute-start(bf16[256,1,4,64]{0,3,2,1:T(8,128)(2,1)S(1)} %get-tuple-element.22), channel_id=1, source_target_pairs={{4,0},{8,4},{12,8},{16,12},{20,16},{24,20},{28,24},{0,28},{5,1},{9... | collective-permute-start | bytes 393224 | tf_op jit(solution)/shard_map/ppermute | solution.py:27
  82.0 3.5 %collective-permute-done.4 = bf16[256,1,4,64]{0,3,2,1:T(8,128)(2,1)S(1)} collective-permute-done((bf16[256,1,4,64]{0,3,2,1:T(8,128)(2,1)S(1)}, bf16[256,1,4,64]{0,3,2,1:T(8,128)(2,1)S(1)}, u32[]{:S(2)}, u32[]{:S(2)}) %collective-permute-start.4) | collective-permute-done | bytes 131104 | tf_op jit(solution)/shard_map/ppermute | solution.py:24
  85.7 3.9 %collective-permute-start.7 = (bf16[256,4,1,64]{0,3,2,1:T(8,128)(2,1)S(1)}, bf16[256,4,1,64]{0,3,2,1:T(8,128)(2,1)S(1)}, u32[]{:S(2)}, u32[]{:S(2)}) collective-permute-start(bf16[256,4,1,64]{0,3,2,1:T(8,128)(2,1)S(1)} %get-tuple-element.20), channel_id=1, source_target_pairs={{1,0},{2,1},{3,2},{0,3},{5,4},{6,5},{7,6},{4,7},{9,8},{10,9},{11,1... | collective-permute-start | bytes 393224 | tf_op jit(solution)/shard_map/ppermute | solution.py:27
  89.5 4.3 %collective-permute-done.6 = bf16[256,4,1,64]{0,3,2,1:T(8,128)(2,1)S(1)} collective-permute-done((bf16[256,4,1,64]{0,3,2,1:T(8,128)(2,1)S(1)}, bf16[256,4,1,64]{0,3,2,1:T(8,128)(2,1)S(1)}, u32[]{:S(2)}, u32[]{:S(2)}) %collective-permute-start.6) | collective-permute-done | bytes 131104 | tf_op jit(solution)/shard_map/ppermute | solution.py:24
  94.5 2.8 %fusion.1 = bf16[768,4,6,64]{0,3,2,1:T(8,128)(2,1)S(1)} fusion(bf16[256,4,1,64]{0,3,2,1:T(8,128)(2,1)S(1)} %collective-permute-done.7, bf16[256,4,1,64]{0,3,2,1:T(8,128)(2,1)S(1)} %collective-permute-done.6, bf16[256,1,4,64]{0,3,2,1:T(8,128)(2,1)S(1)} %collective-permute-done.5, bf16[256,2,4,64]{0,3,2,1:T(8,128)(2,1)S(1)} %fusion.124, ...), kind=kLoop, calls=%fused_computation.5 | loop fusion | flops 40108032 | bytes 4694016 | tf_op jit(solution)/shard_map/concatenate | solution.py:37
  97.3 1.2 fusion.128
  98.5 1.2 fusion.130
  99.7 1.2 fusion.132
  101.0 1.2 fusion.134
  102.2 1.2 fusion.136
  103.4 1.2 fusion.138
  104.6 1.2 fusion.140
  105.8 1.2 fusion.142
  107.0 4.8 %convolution_bitcast_fusion = f32[64,2,2,4,2,64,2]{0,5,6,4,2,3,1:T(8,128)} fusion(f32[2,4,64,256]{3,2,1,0:T(8,128)} %fusion.128, f32[2,4,64,256]{3,2,1,0:T(8,128)} %fusion.130, f32[2,4,64,256]{3,2,1,0:T(8,128)} %fusion.132, f32[2,4,64,256]{3,2,1,0:T(8,128)} %fusion.134, f32[2,4,64,256]{3,2,1,0:T(8,128)} %fusion.136, f32[2,4,64,256]{3,2,1,0:T(8,128)} %fusion.138, ...), kind=kOutput, calls=%fused_computation.16 | convolution fusion | flops 336986112 | bytes 8257536 | tf_op jit(solution)/shard_map/abkoc,czyx->ozaybxk/dot_general | solution.py:194
  111.8 3.3 %copy.24 = f32[64,2,2,4,2,64,2]{0,6,5,4,3,2,1:T(2,128)S(1)} copy(f32[64,2,2,4,2,64,2]{0,5,6,4,2,3,1:T(8,128)} %convolution_bitcast_fusion) | data formatting | bytes 2097152 | tf_op jit(solution)/shard_map/abkoc,czyx->ozaybxk/transpose | solution.py:194
  115.1 1.6 %copy.25 = f32[64,4,8,128]{3,0,2,1:T(8,128)} copy(f32[64,4,8,128]{0,3,2,1:T(8,128)S(1)} %bitcast.344) | data formatting | bytes 2097152 | tf_op jit(solution)/shard_map/reshape | solution.py:196
  116.7 1.4 add_convert_fusion
  118.1 2.6 %collective-permute-start.9 = (bf16[64,1,8,128]{3,0,2,1:T(8,128)(2,1)S(1)}, bf16[64,1,8,128]{3,0,2,1:T(8,128)(2,1)S(1)}, u32[]{:S(2)}, u32[]{:S(2)}) collective-permute-start(bf16[64,1,8,128]{3,0,2,1:T(8,128)(2,1)S(1)} %get-tuple-element.18), channel_id=1, source_target_pairs={{4,0},{8,4},{12,8},{16,12},{20,16},{24,20},{28,24},{0,28},{5,1},{9... | collective-permute-start | bytes 393224 | tf_op jit(solution)/shard_map/ppermute | solution.py:27
  120.8 2.7 %collective-permute-done.8 = bf16[64,1,8,128]{3,0,2,1:T(8,128)(2,1)S(1)} collective-permute-done((bf16[64,1,8,128]{3,0,2,1:T(8,128)(2,1)S(1)}, bf16[64,1,8,128]{3,0,2,1:T(8,128)(2,1)S(1)}, u32[]{:S(2)}, u32[]{:S(2)}) %collective-permute-start.8) | collective-permute-done | bytes 131104 | tf_op jit(solution)/shard_map/ppermute | solution.py:24
  123.5 3.2 %collective-permute-start.10 = (bf16[64,6,1,128]{3,0,2,1:T(8,128)(2,1)S(1)}, bf16[64,6,1,128]{3,0,2,1:T(8,128)(2,1)S(1)}, u32[]{:S(2)}, u32[]{:S(2)}) collective-permute-start(bf16[64,6,1,128]{3,0,2,1:T(8,128)(2,1)S(1)} %get-tuple-element.13), channel_id=1, source_target_pairs={{0,1},{1,2},{2,3},{3,0},{4,5},{5,6},{6,7},{7,4},{8,9},{9,10},{10,1... | collective-permute-start | bytes 294920 | tf_op jit(solution)/shard_map/ppermute | solution.py:24
  127.4 2.7 %collective-permute-done.10 = bf16[64,6,1,128]{3,0,2,1:T(8,128)(2,1)S(1)} collective-permute-done((bf16[64,6,1,128]{3,0,2,1:T(8,128)(2,1)S(1)}, bf16[64,6,1,128]{3,0,2,1:T(8,128)(2,1)S(1)}, u32[]{:S(2)}, u32[]{:S(2)}) %collective-permute-start.10) | collective-permute-done | bytes 98336 | tf_op jit(solution)/shard_map/ppermute | solution.py:24
  130.2 1.8 %collective-permute-done.11 = bf16[64,6,1,128]{3,0,2,1:T(8,128)(2,1)S(1)} collective-permute-done((bf16[64,6,1,128]{3,0,2,1:T(8,128)(2,1)S(1)}, bf16[64,6,1,128]{3,0,2,1:T(8,128)(2,1)S(1)}, u32[]{:S(2)}, u32[]{:S(2)}) %collective-permute-start.11) | collective-permute-done | bytes 98336 | tf_op jit(solution)/shard_map/ppermute | solution.py:27
  133.1 2.4 %maximum_maximum_fusion.1 = bf16[192,6,10,128]{3,0,2,1:T(8,128)(2,1)S(1)} fusion(bf16[64,6,10,1]{3,0,2,1:T(8,128)(2,1)S(1)} %get-tuple-element.6, bf16[64,6,10,127]{3,0,2,1:T(8,128)(2,1)S(1)} %get-tuple-element.8, bf16[64,6,1,128]{3,0,2,1:T(8,128)(2,1)S(1)} %collective-permute-done.11, bf16[64,1,8,128]{3,0,2,1:T(8,128)(2,1)S(1)} %collective-permute-done.9, ...), kind=kLoop, calls=%fused_computation.1 | loop fusion | flops 26542080 | bytes 5898240 | tf_op jit(solution)/shard_map/concatenate | solution.py:37
  135.6 1.4 fusion.5
  137.0 1.4 fusion.7
  138.3 1.4 fusion.9
  139.7 1.4 fusion.11
  141.1 1.4 fusion.13
  142.5 1.4 fusion.15
  143.9 1.4 fusion.17
  145.3 1.5 fusion.19
  146.7 4.9 %fusion.116 = f32[3,4,8,128]{3,0,2,1:T(4,128)} fusion(f32[4,8,128,64]{2,3,1,0:T(8,128)} %fusion.5, f32[4,8,128,64]{2,3,1,0:T(8,128)} %fusion.7, f32[4,8,128,64]{2,3,1,0:T(8,128)} %fusion.9, f32[4,8,128,64]{2,3,1,0:T(8,128)} %fusion.11, f32[4,8,128,64]{2,3,1,0:T(8,128)} %fusion.13, f32[4,8,128,64]{2,3,1,0:T(8,128)} %fusion.15, ...), kind=kOutput, calls=%fused_computation.86 | convolution fusion | flops 105119744 | bytes 10044416 | tf_op jit(solution)/shard_map/oc,czyx->ozyx/dot_general | solution.py:200
  151.6 1.5 copy.26
  (66 shorter events, 12.8 us)
Async XLA Ops:
  0.0 107.0 %copy-start = (bf16[2,2,2,64,256]{4,3,2,1,0:T(8,128)(2,1)S(1)}, bf16[2,2,2,64,256]{4,3,2,1,0:T(8,128)(2,1)}, u32[]{:S(2)}) copy-start(bf16[2,2,2,64,256]{4,3,2,1,0:T(8,128)(2,1)} %param.21) | copy-start | bytes 786436
  0.7 0.8 copy-start.1
  1.5 0.7 copy-start.2
  2.3 0.7 copy-start.3
  3.0 0.7 copy-start.4
  43.5 23.0 %copy-start.8 = (bf16[3,3,64,18]{2,3,1,0:T(8,128)(2,1)S(1)}, bf16[3,3,64,18]{2,3,1,0:T(8,128)(2,1)}, u32[]{:S(2)}) copy-start(bf16[3,3,64,18]{2,3,1,0:T(8,128)(2,1)} %param.17) | copy-start | bytes 62212
  55.2 4.3 %collective-permute-start = (bf16[6,2,8,128]{3,0,2,1:T(8,128)(2,1)S(1)}, bf16[6,2,8,128]{3,0,2,1:T(8,128)(2,1)S(1)}, u32[]{:S(2)}, u32[]{:S(2)}) collective-permute-start(bf16[6,2,8,128]{3,0,2,1:T(8,128)(2,1)S(1)} %get-tuple-element.29), channel_id=1, source_target_pairs={{0,4},{4,8},{8,12},{12,16},{16,20},{20,24},{24,28},{28,0},{1,5},{5... | collective-permute-start | bytes 73736 | tf_op jit(solution)/shard_map/ppermute | solution.py:24
  55.3 4.2 %collective-permute-start.1 = (bf16[6,2,8,128]{3,0,2,1:T(8,128)(2,1)S(1)}, bf16[6,2,8,128]{3,0,2,1:T(8,128)(2,1)S(1)}, u32[]{:S(2)}, u32[]{:S(2)}) collective-permute-start(bf16[6,2,8,128]{3,0,2,1:T(8,128)(2,1)S(1)} %get-tuple-element.30), channel_id=1, source_target_pairs={{4,0},{8,4},{12,8},{16,12},{20,16},{24,20},{28,24},{0,28},{5,1},{9... | collective-permute-start | bytes 73736 | tf_op jit(solution)/shard_map/ppermute | solution.py:27
  59.5 6.0 %collective-permute-start.2 = (bf16[6,8,2,128]{3,0,2,1:T(8,128)(2,1)S(1)}, bf16[6,8,2,128]{3,0,2,1:T(8,128)(2,1)S(1)}, u32[]{:S(2)}, u32[]{:S(2)}) collective-permute-start(bf16[6,8,2,128]{3,0,2,1:T(8,128)(2,1)S(1)} %get-tuple-element.27), channel_id=1, source_target_pairs={{0,1},{1,2},{2,3},{3,0},{4,5},{5,6},{6,7},{7,4},{8,9},{9,10},{10,1... | collective-permute-start | bytes 73736 | tf_op jit(solution)/shard_map/ppermute | solution.py:24
  60.7 4.8 %collective-permute-start.3 = (bf16[6,8,2,128]{3,0,2,1:T(8,128)(2,1)S(1)}, bf16[6,8,2,128]{3,0,2,1:T(8,128)(2,1)S(1)}, u32[]{:S(2)}, u32[]{:S(2)}) collective-permute-start(bf16[6,8,2,128]{3,0,2,1:T(8,128)(2,1)S(1)} %get-tuple-element.28), channel_id=1, source_target_pairs={{1,0},{2,1},{3,2},{0,3},{5,4},{6,5},{7,6},{4,7},{9,8},{10,9},{11,1... | collective-permute-start | bytes 73736 | tf_op jit(solution)/shard_map/ppermute | solution.py:27
  72.3 1.9 %copy-start.6 = (bf16[3,3,64,192]{3,2,1,0:T(8,128)(2,1)S(1)}, bf16[3,3,64,192]{3,2,1,0:T(8,128)(2,1)}, u32[]{:S(2)}) copy-start(bf16[3,3,64,192]{3,2,1,0:T(8,128)(2,1)} %param.18) | copy-start | bytes 663556
  77.5 1.3 copy-start.10
  79.2 6.4 %collective-permute-start.4 = (bf16[256,1,4,64]{0,3,2,1:T(8,128)(2,1)S(1)}, bf16[256,1,4,64]{0,3,2,1:T(8,128)(2,1)S(1)}, u32[]{:S(2)}, u32[]{:S(2)}) collective-permute-start(bf16[256,1,4,64]{0,3,2,1:T(8,128)(2,1)S(1)} %get-tuple-element.21), channel_id=1, source_target_pairs={{0,4},{4,8},{8,12},{12,16},{16,20},{20,24},{24,28},{28,0},{1,5},{5... | collective-permute-start | bytes 393224 | tf_op jit(solution)/shard_map/ppermute | solution.py:24
  79.4 6.2 %collective-permute-start.5 = (bf16[256,1,4,64]{0,3,2,1:T(8,128)(2,1)S(1)}, bf16[256,1,4,64]{0,3,2,1:T(8,128)(2,1)S(1)}, u32[]{:S(2)}, u32[]{:S(2)}) collective-permute-start(bf16[256,1,4,64]{0,3,2,1:T(8,128)(2,1)S(1)} %get-tuple-element.22), channel_id=1, source_target_pairs={{4,0},{8,4},{12,8},{16,12},{20,16},{24,20},{28,24},{0,28},{5,1},{9... | collective-permute-start | bytes 393224 | tf_op jit(solution)/shard_map/ppermute | solution.py:27
  85.6 8.2 %collective-permute-start.6 = (bf16[256,4,1,64]{0,3,2,1:T(8,128)(2,1)S(1)}, bf16[256,4,1,64]{0,3,2,1:T(8,128)(2,1)S(1)}, u32[]{:S(2)}, u32[]{:S(2)}) collective-permute-start(bf16[256,4,1,64]{0,3,2,1:T(8,128)(2,1)S(1)} %get-tuple-element.19), channel_id=1, source_target_pairs={{0,1},{1,2},{2,3},{3,0},{4,5},{5,6},{6,7},{7,4},{8,9},{9,10},{10,1... | collective-permute-start | bytes 393224 | tf_op jit(solution)/shard_map/ppermute | solution.py:24
  85.7 8.2 %collective-permute-start.7 = (bf16[256,4,1,64]{0,3,2,1:T(8,128)(2,1)S(1)}, bf16[256,4,1,64]{0,3,2,1:T(8,128)(2,1)S(1)}, u32[]{:S(2)}, u32[]{:S(2)}) collective-permute-start(bf16[256,4,1,64]{0,3,2,1:T(8,128)(2,1)S(1)} %get-tuple-element.20), channel_id=1, source_target_pairs={{1,0},{2,1},{3,2},{0,3},{5,4},{6,5},{7,6},{4,7},{9,8},{10,9},{11,1... | collective-permute-start | bytes 393224 | tf_op jit(solution)/shard_map/ppermute | solution.py:27
  94.5 2.9 %copy-start.5 = (bf16[3,3,256,768]{3,2,1,0:T(8,128)(2,1)S(1)}, bf16[3,3,256,768]{3,2,1,0:T(8,128)(2,1)}, u32[]{:S(2)}) copy-start(bf16[3,3,256,768]{3,2,1,0:T(8,128)(2,1)} %param.20) | copy-start | bytes 10616836
  118.1 5.4 %collective-permute-start.8 = (bf16[64,1,8,128]{3,0,2,1:T(8,128)(2,1)S(1)}, bf16[64,1,8,128]{3,0,2,1:T(8,128)(2,1)S(1)}, u32[]{:S(2)}, u32[]{:S(2)}) collective-permute-start(bf16[64,1,8,128]{3,0,2,1:T(8,128)(2,1)S(1)} %get-tuple-element.17), channel_id=1, source_target_pairs={{0,4},{4,8},{8,12},{12,16},{16,20},{20,24},{24,28},{28,0},{1,5},{5... | collective-permute-start | bytes 393224 | tf_op jit(solution)/shard_map/ppermute | solution.py:24
  118.1 5.4 %collective-permute-start.9 = (bf16[64,1,8,128]{3,0,2,1:T(8,128)(2,1)S(1)}, bf16[64,1,8,128]{3,0,2,1:T(8,128)(2,1)S(1)}, u32[]{:S(2)}, u32[]{:S(2)}) collective-permute-start(bf16[64,1,8,128]{3,0,2,1:T(8,128)(2,1)S(1)} %get-tuple-element.18), channel_id=1, source_target_pairs={{4,0},{8,4},{12,8},{16,12},{20,16},{24,20},{28,24},{0,28},{5,1},{9... | collective-permute-start | bytes 393224 | tf_op jit(solution)/shard_map/ppermute | solution.py:27
  123.5 6.6 %collective-permute-start.10 = (bf16[64,6,1,128]{3,0,2,1:T(8,128)(2,1)S(1)}, bf16[64,6,1,128]{3,0,2,1:T(8,128)(2,1)S(1)}, u32[]{:S(2)}, u32[]{:S(2)}) collective-permute-start(bf16[64,6,1,128]{3,0,2,1:T(8,128)(2,1)S(1)} %get-tuple-element.13), channel_id=1, source_target_pairs={{0,1},{1,2},{2,3},{3,0},{4,5},{5,6},{6,7},{7,4},{8,9},{9,10},{10,1... | collective-permute-start | bytes 294920 | tf_op jit(solution)/shard_map/ppermute | solution.py:24
  126.7 5.3 %collective-permute-start.11 = (bf16[64,6,1,128]{3,0,2,1:T(8,128)(2,1)S(1)}, bf16[64,6,1,128]{3,0,2,1:T(8,128)(2,1)S(1)}, u32[]{:S(2)}, u32[]{:S(2)}) collective-permute-start(bf16[64,6,1,128]{3,0,2,1:T(8,128)(2,1)S(1)} %get-tuple-element.14), channel_id=1, source_target_pairs={{1,0},{2,1},{3,2},{0,3},{5,4},{6,5},{7,6},{4,7},{9,8},{10,9},{11,1... | collective-permute-start | bytes 294920 | tf_op jit(solution)/shard_map/ppermute | solution.py:27
  133.1 2.4 %copy-start.7 = (bf16[3,3,64,192]{3,2,1,0:T(8,128)(2,1)S(1)}, bf16[3,3,64,192]{3,2,1,0:T(8,128)(2,1)}, u32[]{:S(2)}) copy-start(bf16[3,3,64,192]{3,2,1,0:T(8,128)(2,1)} %param.22) | copy-start | bytes 663556
  143.9 2.9 %copy-start.9 = (bf16[3,64]{1,0:T(4,128)(2,1)S(1)}, bf16[3,64]{1,0:T(4,128)(2,1)}, u32[]{:S(2)}) copy-start(bf16[3,64]{1,0:T(4,128)(2,1)} %param.23) | copy-start | bytes 1156

commit v2 on v1

--- a/solution.py
+++ b/solution.py
@@ -15,38 +15,414 @@
 slope = 0.1
 
 
-def with_halo(block, sides, width):
-    for axis, dim in sides:
-        count = lax.axis_size(axis)
-        forward = [(i, i + 1) for i in range(count - 1)]
-        forward.append((count - 1, 0))
-        backward = [(target, source) for source, target in forward]
-        low = lax.ppermute(
-            lax.slice_in_dim(block, block.shape[dim] - width, None, axis=dim), axis, forward
-        )
-        high = lax.ppermute(lax.slice_in_dim(block, 0, width, axis=dim), axis, backward)
-        block = jnp.concatenate([low, block, high], axis=dim)
-    return block
+BF16 = jnp.bfloat16
+F32 = jnp.float32
+MESH = pl.DeviceIdType.MESH
+SIDES = [(dz, dy) for dz in (-1, 0, 1) for dy in (-1, 0, 1) if dz or dy]
 
 
 def act(values):
     return jnp.maximum(values, slope * values)
 
 
-def conv_rim(padded, weight):
-    stacked = jnp.concatenate([jnp.roll(padded, 1, 3), padded, jnp.roll(padded, -1, 3)], 0)
-    out_z = padded.shape[1] - 2
-    out_y = padded.shape[2] - 2
-    total = jnp.zeros((weight.shape[2], out_z, out_y, padded.shape[3]), jnp.float32)
-    for a in range(3):
+def dot(left, right):
+    return jnp.dot(left, right, preferred_element_type=F32)
+
+
+def neighbour(dz, dy):
+    slabs, tiles = lax.axis_size("slab"), lax.axis_size("tile")
+    return (
+        lax.rem(lax.axis_index("slab") + (dz + slabs), slabs),
+        lax.rem(lax.axis_index("tile") + (dy + tiles), tiles),
+    )
+
+
+def greet(devices):
+    barrier = pltpu.get_barrier_semaphore()
+    for device in devices:
+        pl.semaphore_signal(barrier, inc=1, device_id=device, device_id_type=MESH)
+    pl.semaphore_wait(barrier, len(devices))
+
+
+def span(shift, size, width):
+    if shift > 0:
+        return pl.ds(size - width, width), pl.ds(0, width)
+    if shift < 0:
+        return pl.ds(0, width), pl.ds(size + width, width)
+    return pl.ds(0, size), pl.ds(width, size)
+
+
+def exchange(block, padded, width, send, recv):
+    planes, rows = block.shape[:2]
+    copies = []
+    for n, (dz, dy) in enumerate(SIDES):
+        from_z, to_z = span(dz, planes, width)
+        from_y, to_y = span(dy, rows, width)
+        copies.append(
+            pltpu.make_async_remote_copy(
+                src_ref=block.at[from_z, from_y],
+                dst_ref=padded.at[to_z, to_y],
+                send_sem=send.at[n],
+                recv_sem=recv.at[n],
+                device_id=neighbour(dz, dy),
+                device_id_type=MESH,
+            )
+        )
+    for copy in copies:
+        copy.start()
+    padded[pl.ds(width, planes), pl.ds(width, rows)] = block[...]
+    for copy in copies:
+        copy.wait()
+
+
+def halo_kernel(width, block, padded, send, recv):
+    greet([neighbour(dz, dy) for dz, dy in SIDES])
+    exchange(block, padded, width, send, recv)
+
+
+def with_halo(block, width, number):
+    planes, rows, depth, lanes = block.shape
+    return pl.pallas_call(
+        functools.partial(halo_kernel, width),
+        in_specs=[pl.BlockSpec(memory_space=pltpu.VMEM)],
+        out_specs=pl.BlockSpec(memory_space=pltpu.VMEM),
+        out_shape=jax.ShapeDtypeStruct(
+            (planes + 2 * width, rows + 2 * width, depth, lanes), block.dtype
+        ),
+        scratch_shapes=[pltpu.SemaphoreType.DMA((8,)), pltpu.SemaphoreType.DMA((8,))],
+        compiler_params=pltpu.CompilerParams(
+            collective_id=number, has_side_effects=True, vmem_limit_bytes=32 << 20
+        ),
+        name=f"halo{number}",
+    )(block)
+
+
+def reduce_kernel(bits, field, padded, *scratch):
+    tiles = lax.axis_size("tile")
+    slab, tile = lax.axis_index("slab"), lax.axis_index("tile")
+    half = tiles // 2
+    mine = [slab // 2**b % 2 for b in range(bits)]
+    partner = [(slab + 2**b * (1 - 2 * mine[b]), tile) for b in range(bits)]
+    ahead = [(slab, lax.rem(tile + d, tiles)) for d in range(1, tiles)]
+    greet(partner + ahead + [neighbour(dz, dy) for dz, dy in SIDES])
+    gets, sums = scratch[: 2 * bits], scratch[2 * bits : 4 * bits]
+    last, block, send, recv, send_z, recv_z, send_h, recv_h, whole = scratch[4 * bits :]
+
+    def start(source, target, sem, device):
+        copy = pltpu.make_async_remote_copy(
+            src_ref=source,
+            dst_ref=target,
+            send_sem=send.at[sem],
+            recv_sem=recv.at[sem],
+            device_id=device,
+            device_id_type=MESH,
+        )
+        copy.start()
+        return copy
+
+    orders = [[0] + list(range(1, bits)), [0] + list(range(bits - 1, 0, -1))]
+    left = [list(range(bits - 1, -1, -1)) for _ in range(2)]
+    here = [None, None]
+    for stage in range(bits):
+        copies = []
+        for h in range(2):
+            b = orders[h][stage]
+            at = (slice(None),) * left[h].index(b)
+            parts = pl.ds(h * half, half)
+            if stage == 0:
+                away = field.at[at + (1 - mine[b], parts)]
+            else:
+                away = here[h].at[at + (1 - mine[b],)]
+            copies.append(start(away, gets[2 * stage + h], 2 * stage + h, partner[b]))
+        for h in range(2):
+            b = orders[h][stage]
+            at = (slice(None),) * left[h].index(b)
+            parts = pl.ds(h * half, half)
+            copies[h].wait()
+            if stage == 0:
+                own = field[at + (mine[b], parts)]
+            else:
+                own = here[h][at + (mine[b],)]
+            total = own.astype(F32) + gets[2 * stage + h][...].astype(F32)
+            sums[2 * stage + h][...] = total.astype(BF16)
+            here[h] = sums[2 * stage + h]
+            left[h].remove(b)
+    whole[pl.ds(0, half)] = here[0][...]
+    whole[pl.ds(half, half)] = here[1][...]
+    copies = []
+    for d in range(1, tiles):
+        copy = pltpu.make_async_remote_copy(
+            src_ref=whole.at[lax.rem(tile + d, tiles)],
+            dst_ref=last.at[d - 1],
+            send_sem=send_z.at[d - 1],
+            recv_sem=recv_z.at[d - 1],
+            device_id=ahead[d - 1],
+            device_id_type=MESH,
+        )
+        copy.start()
+        copies.append(copy)
+    total = whole[tile].astype(F32)
+    for d in range(1, tiles):
+        copies[d - 1].wait()
+        total = total + last[d - 1].astype(F32)
+    total = total.astype(BF16).astype(F32)
+    block[...] = jnp.zeros_like(block)
+    for c in range(total.shape[0]):
+        for z in range(CZ):
+            block[z, :, c, :] = total[c, z * YT : (z + 1) * YT]
+    exchange(block, padded, 2, send_h, recv_h)
+
+
+def reduce_field(field):
+    slabs, tiles, attrs, size, lanes = field.shape
+    bits = slabs.bit_length() - 1
+    half = tiles // 2
+    parts = []
+    for stage in range(bits):
+        shape = (2,) * (bits - 1 - stage) + (half, attrs, size, lanes)
+        parts += [pltpu.VMEM(shape, BF16)] * 2
+    scratch = parts + parts
+    scratch += [
+        pltpu.VMEM((tiles - 1, attrs, size, lanes), BF16),
+        pltpu.VMEM((CZ, YT, 8, lanes), F32),
+        pltpu.SemaphoreType.DMA((2 * bits,)),
+        pltpu.SemaphoreType.DMA((2 * bits,)),
+        pltpu.SemaphoreType.DMA((tiles - 1,)),
+        pltpu.SemaphoreType.DMA((tiles - 1,)),
+        pltpu.SemaphoreType.DMA((8,)),
+        pltpu.SemaphoreType.DMA((8,)),
+        pltpu.VMEM((tiles, attrs, size, lanes), BF16),
+    ]
+    return pl.pallas_call(
+        functools.partial(reduce_kernel, bits),
+        in_specs=[pl.BlockSpec(memory_space=pltpu.VMEM)],
+        out_specs=pl.BlockSpec(memory_space=pltpu.VMEM),
+        out_shape=jax.ShapeDtypeStruct((CZ + 4, YT + 4, 8, lanes), F32),
+        scratch_shapes=scratch,
+        compiler_params=pltpu.CompilerParams(
+            collective_id=0, has_side_effects=True, vmem_limit_bytes=56 << 20
+        ),
+        name="reduce_field",
+    )(field.reshape((2,) * bits + field.shape[1:]))
+
+
+def spread(values):
+    return jnp.concatenate(
+        [pltpu.roll(values, 1, 1), values, pltpu.roll(values, NX - 1, 1)], 0
+    ).astype(BF16)
+
+
+def conv_rows(stack, weight, acc):
+    planes, rows = stack.shape[0] - 2, stack.shape[1] - 2
+    outs = weight.shape[2]
+    lefts = [jnp.concatenate([weight[a, b] for a in range(3)], 0) for b in range(3)]
+    for z in range(planes + 2):
+        for j in range(rows // 2):
+            part = None
+            for b in range(3):
+                y = 2 * j + b
+                pair = jnp.concatenate([stack[z, y], stack[z, y + 1]], 1)
+                term = dot(lefts[b], pair)
+                part = term if part is None else part + term
+            for a in range(3):
+                if 0 <= z - a < planes:
+                    piece = part[a * outs : (a + 1) * outs]
+                    if a == 0:
+                        acc[z, j] = piece
+                    else:
+                        acc[z - a, j] += piece
+
+
+def lane_index(rows):
+    return lax.broadcasted_iota(jnp.int32, (rows, 128), 1)
+
+
+def fine_kernel(grid, lift, fine, down, second, lowered, wide, stack, acc):
+    planes, rows = grid.shape[0] - 2, grid.shape[1] - 2
+    for z in range(planes + 2):
+        block = grid[z]
+        wide[z, :, 0:8] = pltpu.roll(block, 1, 2)
+        wide[z, :, 8:16] = block
+        wide[z, :, 16:24] = pltpu.roll(block, NX - 1, 2)
+
+    def lift_plane(z, carry):
+        for y in range(0, rows, 2):
+            pair = jnp.concatenate(
+                [
+                    jnp.concatenate(
+                        [wide[z + a, y + s + b] for a in range(3) for b in range(3)], 0
+                    ).astype(BF16)
+                    for s in range(2)
+                ],
+                1,
+            )
+            values = act(dot(lift[...], pair))
+            stack[z, y] = spread(values[:, :NX])
+            stack[z, y + 1] = spread(values[:, NX:])
+        return carry
+
+    lax.fori_loop(0, planes, lift_plane, 0)
+    conv_rows(stack, fine, acc)
+    for z in range(CZ):
+        for j in range(YT // 2):
+            values = act(acc[z, j]).astype(BF16)
+            second[z, 2 * j] = values[:, :NX]
+            second[z, 2 * j + 1] = values[:, NX:]
+    source = lax.broadcasted_iota(jnp.int32, (NX, NX), 0)
+    target = lax.broadcasted_iota(jnp.int32, (NX, NX), 1)
+    half = NX // 2
+    parity = jnp.where(target < half, 0, 1)
+    sel = jnp.where(source == 2 * (target - half * parity) + parity, 1.0, 0.0).astype(BF16)
+    chans = down.shape[0] // 2
+    lane = lane_index(chans // 2)
+    for z in range(CZ // 2):
+        for j in range(YT // 4):
+            pair = []
+            for y in (2 * j, 2 * j + 1):
+                tall = jnp.concatenate(
+                    [second[2 * z + a, 2 * y + b] for a in range(2) for b in range(2)], 0
+                )
+                pair.append(dot(tall, sel).astype(BF16))
+            out = dot(down[...], jnp.concatenate(pair, 1))
+            for s in range(2):
+                q = out[:, s * NX : (s + 1) * NX]
+                h = chans // 2
+                q00, q01, q10, q11 = (q[i * h : (i + 1) * h] for i in range(4))
+                row = jnp.where(lane < half, q00, q11) + pltpu.roll(
+                    jnp.where(lane < half, q01, q10), half, 1
+                )
+                lowered[z, 2 * j + s] = act(row).astype(BF16)
+
+
+def fine_level(grid, lift, fine, down):
+    outs, chans = fine.shape[2], down.shape[3]
+    planes, rows = grid.shape[0] - 2, grid.shape[1] - 2
+    wide = lift.reshape(3, 3, outs, 3, -1)
+    wide = jnp.pad(wide, ((0, 0),) * 4 + ((0, 8 - wide.shape[4]),))
+    wide = wide.transpose(2, 0, 1, 3, 4).reshape(outs, -1)
+    low = down.transpose(2, 3, 0, 1, 4).reshape(2 * chans, 4 * outs)
+    return pl.pallas_call(
+        fine_kernel,
+        out_shape=(
+            jax.ShapeDtypeStruct((CZ, YT, outs, NX), BF16),
+            jax.ShapeDtypeStruct((CZ // 2, YT // 2, chans // 2, NX), BF16),
+        ),
+        scratch_shapes=[
+            pltpu.VMEM((planes + 2, rows + 2, 24, NX), F32),
+            pltpu.VMEM((planes, rows, 3 * outs, NX), BF16),
+            pltpu.VMEM((CZ, YT // 2, outs, 2 * NX), F32),
+        ],
+        compiler_params=pltpu.CompilerParams(vmem_limit_bytes=48 << 20),
+        name="fine_level",
+    )(grid, wide, fine, low)
+
+
+def coarse_kernel(low, weight, up, second, joined, acc):
+    half = NX // 2
+    chans = weight.shape[2]
+    outs = up.shape[3]
+    lane = lane_index(chans // 2)
+    planes = low.shape[0]
+    for z in range(planes):
+        row = [low[z, y].astype(F32) for y in range(low.shape[1])]
+        turned = [pltpu.roll(r, half, 1) for r in row]
+        pairs = []
+        for r in range(len(row) - 1):
+            top = jnp.where(lane < half, row[r], turned[r + 1])
+            bottom = jnp.where(lane < half, turned[r], row[r + 1])
+            pairs.append(jnp.concatenate([top, bottom], 0).astype(BF16))
         for b in range(3):
-            total = total + jnp.einsum(
-                "oi,izyx->ozyx",
-                weight[a, b],
-                stacked[:, a : a + out_z, b : b + out_y],
-                preferred_element_type=jnp.float32,
+            right = jnp.concatenate([pairs[b], pairs[2 + b]], 1)
+            for a in range(3):
+                if 0 <= z - a < planes - 2:
+                    for k in range(3):
+                        part = dot(weight[a, b, :, k * chans : (k + 1) * chans], right)
+                        if a == 0 and b == 0:
+                            acc[z - a, k] = part
+                        else:
+                            acc[z - a, k] += part
+    source = lax.broadcasted_iota(jnp.int32, (NX, 4 * NX), 0)
+    target = lax.broadcasted_iota(jnp.int32, (NX, 4 * NX), 1)
+    spot = target % NX
+    want = target // (2 * NX) * half + spot // 2
+    sel = jnp.where((source == want) & (spot % 2 == target // NX % 2), 1.0, 0.0).astype(BF16)
+    lane = lane_index(chans)
+    lefts = [
+        jnp.concatenate([up[a, b, k] for a in range(2) for b in range(2)], 0) for k in range(2)
+    ]
+    for z in range(planes - 2):
+        for j in range(2):
+            at = slice(j * NX, (j + 1) * NX)
+            before, same, after = (acc[z, k, :, at] for k in range(3))
+            before = jnp.where(
+                lane % half == 0, pltpu.roll(before, half + 1, 1), pltpu.roll(before, 1, 1)
             )
-    return total
+            after = jnp.where(
+                lane % half == half - 1,
+                pltpu.roll(after, half - 1, 1),
+                pltpu.roll(after, NX - 1, 1),
+            )
+            coarse = act(before + same + after).astype(BF16)
+            wide = dot(coarse, sel).astype(BF16)
+            right = [
+                jnp.concatenate([wide[:, k * NX : (k + 1) * NX], wide[:, (2 + k) * NX : (3 + k) * NX]], 1)
+                for k in range(2)
+            ]
+            raised = dot(lefts[0], right[0]) + dot(lefts[1], right[1])
+            for a in range(2):
+                for b in range(2):
+                    for p in range(2):
+                        y = 2 * (2 * j + p) + b
+                        piece = raised[
+                            (2 * a + b) * outs : (2 * a + b + 1) * outs, p * NX : (p + 1) * NX
+                        ]
+                        joined[2 * z + a, y] = (second[2 * z + a, y].astype(F32) + piece).astype(
+                            BF16
+                        )
+
+
+def coarse_level(low, weight, up, second):
+    chans = weight.shape[2]
+    return pl.pallas_call(
+        coarse_kernel,
+        out_shape=jax.ShapeDtypeStruct(second.shape, BF16),
+        scratch_shapes=[pltpu.VMEM((CZ // 2, 3, chans, 2 * NX), F32)],
+        compiler_params=pltpu.CompilerParams(vmem_limit_bytes=48 << 20),
+        name="coarse_level",
+    )(low, weight, up, second)
+
+
+def merge_kernel(joined, weight, head, out, stack, acc):
+    planes, rows = joined.shape[:2]
+
+    def widen(z, carry):
+        for y in range(rows):
+            stack[z, y] = spread(joined[z, y].astype(F32))
+        return carry
+
+    lax.fori_loop(0, planes, widen, 0)
+    conv_rows(stack, weight, acc)
+    for z in range(planes - 2):
+        for j in range(rows // 2 - 1):
+            moved = dot(head[...], act(acc[z, j]).astype(BF16))
+            for s in range(2):
+                out[:, z, 2 * j + s, :] = moved[: out.shape[0], s * NX : (s + 1) * NX]
+
+
+def merge_level(joined, weight, head):
+    planes, rows, chans, lanes = joined.shape
+    final = head.shape[0]
+    padded = jnp.pad(head, ((0, 16 - final), (0, 0)))
+    return pl.pallas_call(
+        merge_kernel,
+        out_shape=jax.ShapeDtypeStruct((final, planes - 2, rows - 2, lanes), F32),
+        scratch_shapes=[
+            pltpu.VMEM((planes, rows, 3 * chans, lanes), BF16),
+            pltpu.VMEM((planes - 2, rows // 2 - 1, chans, 2 * lanes), F32),
+        ],
+        compiler_params=pltpu.CompilerParams(vmem_limit_bytes=48 << 20),
+        name="merge_level",
+    )(joined, weight, padded)
 
 
 GROUP = 4
@@ -176,28 +552,12 @@
     field = deposit(
         particle_features, destination, cell_index, offset_code, live_count, slabs, tiles
     )
-    field = lax.all_to_all(field, "slab", split_axis=0, concat_axis=0, tiled=True)
-    field = jnp.sum(field.astype(jnp.float32), 0).astype(jnp.bfloat16)
-    field = lax.all_to_all(field, "tile", split_axis=0, concat_axis=0, tiled=True)
-    grid = jnp.sum(field.astype(jnp.float32), 0).astype(jnp.bfloat16)
-    grid = grid.reshape(grid.shape[0], CZ, YT, NX)
-    padded = with_halo(grid, (("slab", 1), ("tile", 2)), 2)
-    first_padded = act(conv_rim(padded, lift_weight)).astype(jnp.bfloat16)
-    second = act(conv_rim(first_padded, fine_weight)).astype(jnp.bfloat16)
-    channels, planes, width_y, width_x = second.shape
-    blocks = second.reshape(channels, planes // 2, 2, width_y // 2, 2, width_x // 2, 2)
-    lowered = act(
-        jnp.einsum("abkoc,czaybxk->ozyx", down_weight, blocks, preferred_element_type=jnp.float32)
-    ).astype(jnp.bfloat16)
-    lowered_padded = with_halo(lowered, (("slab", 1), ("tile", 2)), 1)
-    coarse = act(conv_rim(lowered_padded, coarse_weight)).astype(jnp.bfloat16)
-    raised = jnp.einsum(
-        "abkoc,czyx->ozaybxk", up_weight, coarse, preferred_element_type=jnp.float32
-    ).reshape(up_weight.shape[3], planes, width_y, width_x)
-    joined = (second.astype(jnp.float32) + raised).astype(jnp.bfloat16)
-    joined_padded = with_halo(joined, (("slab", 1), ("tile", 2)), 1)
-    merged = act(conv_rim(joined_padded, merge_weight)).astype(jnp.bfloat16)
-    return jnp.einsum("oc,czyx->ozyx", head_weight, merged, preferred_element_type=jnp.float32)
+    grid = reduce_field(field)
+    second, lowered = fine_level(grid, lift_weight, fine_weight, down_weight)
+    lowered = with_halo(lowered, 1, 1)
+    joined = coarse_level(lowered, coarse_weight, up_weight, second)
+    joined = with_halo(joined, 1, 2)
+    return merge_level(joined, merge_weight, head_weight)
 
 
 def solution(mesh):

time: 154 us -> 97.6 us (0.63)
  Pallas kernels: 13.6 us -> 78.7 us
  matrix products: 39.8 us -> 0 us
  blocking collectives: 37.6 us -> 0 us
  starting transfers between devices: 19.9 us -> 0 us
  waiting for transfers between devices: 18.9 us -> 0 us
  other arithmetic: 9.73 us -> 0 us
  local copies, waits for them, and re-layouts: 12.4 us -> 17.3 us
    pallas_call x0 -> x6, Pallas kernels: none -> 65.1 us  [the longest x1 31.3 us: reduce_field(): pl.pallas_call(functools.partial(reduce_kernel, bits), in_specs=[pl.Block...]
    dot_general x37 -> x0, matrix products: 39.8 us -> none  [the longest x34 29.8 us: conv_rim(): jnp.einsum('oi,izyx->ozyx', weight[a, b], stacked[:, a:a + out_z, b:b + o...]
    all_to_all x2 -> x0, blocking collectives: 37.6 us -> none  [the longest x1 25.9 us: body(): lax.all_to_all(field, 'slab', split_axis=0, concat_axis=0, tiled=True)]
    ppermute x12 -> x0, starting transfers between devices: 19.9 us -> none  [the longest x6 15.2 us: with_halo(): lax.ppermute(lax.slice_in_dim(block, 0, width, axis=dim), axis, backward)]
    ppermute x12 -> x0, waiting for transfers between devices: 18.9 us -> none  [the longest x6 17 us: with_halo(): lax.ppermute(lax.slice_in_dim(block, block.shape[dim] - width, None, axis...]
    concatenate x7 -> x0, other arithmetic: 7.99 us -> none  [the longest x4 7.64 us: conv_rim(): jnp.concatenate([jnp.roll(padded, 1, 3), padded, jnp.roll(padded, -1, 3)]...]
    unnamed x22 -> x26, local copies, waits for them, and re-layouts: 3.02 us -> 8.76 us
    reshape x1 -> x4, local copies, waits for them, and re-layouts: 1.58 us -> 7.1 us  [the longest x2 4.12 us: fine_level(): low = down.transpose(2, 3, 0, 1, 4).reshape(2 * chans, 4 * outs)]
  transfers between devices with their start and end apart: 12 -> 0, of which waited for: 7 -> 0; matrix products, arithmetic and copies ran while one was open for 0% -> 0% of each run, Pallas kernels for 0% -> 0%
where the time goes in v2:
time: 97.6 us; the launch traced here: 96.8 us
  Pallas kernels  78.7 us (81%)
  local copies, waits for them, and re-layouts  17.3 us (18%)
    pallas_call x1, Pallas kernels, reduce_field(): pl.pallas_call(functools.partial(reduce_kernel, bits), in_specs=[pl.Block...  31.3 us
    pallas_call x2, Pallas kernels, with_halo(): pl.pallas_call(functools.partial(halo_kernel, width), in_specs=[pl.BlockS...  21.6 us
    pallas_call x1, Pallas kernels, deposit(): pl.pallas_call(functools.partial(deposit_kernel, slabs, tiles), grid=(sla...  13.6 us
    unnamed x26, local copies, waits for them, and re-layouts  8.76 us
    pallas_call x1, Pallas kernels, fine_level(): pl.pallas_call(fine_kernel, out_shape=(jax.ShapeDtypeStruct((CZ, YT, outs...  4.99 us
    reshape x2, local copies, waits for them, and re-layouts, fine_level(): low = down.transpose(2, 3, 0, 1, 4).reshape(2 * chans, 4 * outs)  4.12 us
    pallas_call x1, Pallas kernels, merge_level(): pl.pallas_call(merge_kernel, out_shape=jax.ShapeDtypeStruct((final, plane...  3.67 us
    pallas_call x1, Pallas kernels, coarse_level(): pl.pallas_call(coarse_kernel, out_shape=jax.ShapeDtypeStruct(second.shape...  3.61 us

profile of v2, /device:TPU:0, one launch (start us, length us, event | category | flops | bytes accessed | tf_op | source)
XLA Modules:
  0.0 96.8 jit_solution(16902521586029403080)
XLA Ops:
  0.7 0.0 copy-start.8
  0.7 0.8 copy-done.8
  1.5 0.0 copy-start.9
  1.5 0.7 copy-done.9
  2.2 0.0 copy-start.10
  2.2 0.7 copy-done.10
  2.9 0.0 copy-start.11
  2.9 0.7 copy-done.11
  3.6 0.0 copy-start.1
  3.6 13.6 %deposit.1 = bf16[8,4,6,32,128]{4,3,2,1,0:T(8,128)(2,1)S(1)} custom-call(bf16[6,4096]{1,0:T(8,128)(2,1)S(1)} %copy-done.8, s32[1,4096]{1,0:T(1,128)S(1)} %bitcast.11, s32[1,4096]{1,0:T(1,128)S(1)} %bitcast.12, s32[1,4096]{1,0:T(1,128)S(1)} %bitcast.13, s32[1]{0:T(128)S(6)} %copy.20.live_ref), custom_call_target="tpu_custom_call" | custom-call | tf_op jit(solution)/shard_map/deposit/pallas_call | solution.py:509
  17.2 0.0 copy-start
  17.2 1.2 %copy-done = bf16[8,4,6,32,128]{4,3,2,1,0:T(8,128)(2,1)} copy-done((bf16[8,4,6,32,128]{4,3,2,1,0:T(8,128)(2,1)}, bf16[8,4,6,32,128]{4,3,2,1,0:T(8,128)(2,1)S(1)}, u32[]{:S(2)}) %copy-start) | copy-done | bytes 1572888
  18.4 31.3 %reduce_field.1.grid = f32[8,12,8,128]{3,2,1,0:T(8,128)} custom-call(bf16[2,2,2,4,6,32,128]{6,5,4,3,2,1,0:T(8,128)(2,1)} %bitcast.10), custom_call_target="tpu_custom_call" | custom-call | tf_op jit(solution)/shard_map/reduce_field/pallas_call | solution.py:196
  49.7 2.0 %copy.18 = bf16[2,256,2,2,64]{4,3,2,1,0:T(2,128)(2,1)} copy(bf16[2,256,2,2,64]{1,4,0,3,2:T(8,128)(2,1)} %bitcast.14) | data formatting | bytes 524288 | tf_op jit(solution)/shard_map/reshape | solution.py:303
  51.6 2.2 %reshape.28.down = bf16[512,256]{1,0:T(8,128)(2,1)} reshape(bf16[2,256,2,2,64]{4,3,2,1,0:T(2,128)(2,1)} %copy.18) | data formatting | bytes 524288 | tf_op jit(solution)/shard_map/reshape | solution.py:303
  53.8 1.5 %reshape.25 = bf16[3,3,64,3,6]{2,4,3,1,0:T(8,128)(2,1)} reshape(bf16[3,3,64,18]{2,3,1,0:T(8,128)(2,1)} %param.17) | data formatting | bytes 41472 | tf_op jit(solution)/shard_map/reshape | solution.py:300
  55.3 1.5 %pad.8 = bf16[3,3,64,3,8]{2,4,3,1,0:T(8,128)(2,1)} pad(bf16[3,3,64,3,6]{2,4,3,1,0:T(8,128)(2,1)} %reshape.25, bf16[]{:T(256)} %constant.2.clone.1), padding=0_0x0_0x0_0x0_0x0_2 | pad | bytes 48386 | tf_op jit(solution)/shard_map/jit(_pad)/pad | solution.py:301
  56.7 1.5 %copy.16.lift = bf16[64,216]{1,0:T(8,128)(2,1)} copy(bf16[64,216]{0,1:T(8,128)(2,1)} %bitcast.15) | data formatting | bytes 55296 | tf_op jit(solution)/shard_map/reshape | solution.py:302
  58.2 0.0 copy-start.2
  58.2 1.0 %copy-done.2 = f32[8,12,8,128]{3,2,1,0:T(8,128)S(1)} copy-done((f32[8,12,8,128]{3,2,1,0:T(8,128)S(1)}, f32[8,12,8,128]{3,2,1,0:T(8,128)}, u32[]{:S(2)}) %copy-start.2) | copy-done | bytes 393240
  59.2 0.0 copy-start.3
  59.2 0.9 copy-done.3
  60.2 0.0 copy-start.4
  60.2 1.0 copy-done.4
  61.1 0.0 copy-start.7
  61.1 0.8 copy-done.7
  61.9 5.0 %fine_level.1 = (bf16[4,8,64,128]{3,2,1,0:T(8,128)(2,1)S(1)}, bf16[2,4,128,128]{3,2,1,0:T(8,128)(2,1)S(1)}) custom-call(f32[8,12,8,128]{3,2,1,0:T(8,128)S(1)} %copy-done.2, bf16[64,216]{1,0:T(8,128)(2,1)S(1)} %copy-done.7, bf16[3,3,64,192]{3,2,1,0:T(8,128)(2,1)S(1)} %copy-done.4, bf16[512,256]{1,0:T(8,128)(2,1)S(1)} %copy-done.3), custom_call_target="tpu_custom_call" | custom-call | tf_op jit(solution)/shard_map/fine_level/pallas_call | solution.py:304
  66.9 12.2 %halo1.1.low = bf16[4,6,128,128]{3,2,1,0:T(8,128)(2,1)S(1)} custom-call(bf16[2,4,128,128]{3,2,1,0:T(8,128)(2,1)S(1)} %get-tuple-element.7.block), custom_call_target="tpu_custom_call" | custom-call | tf_op jit(solution)/shard_map/halo1/pallas_call | solution.py:85
  79.1 0.0 copy-done.1
  79.1 0.0 copy-start.6
  79.2 0.9 copy-done.6
  80.1 0.0 copy-start.12
  80.1 0.0 copy-start.5
  80.1 3.6 %coarse_level.1.block = bf16[4,8,64,128]{3,2,1,0:T(8,128)(2,1)S(1)} custom-call(bf16[4,6,128,128]{3,2,1,0:T(8,128)(2,1)S(1)} %halo1.1.low, bf16[3,3,256,768]{3,2,1,0:T(8,128)(2,1)S(1)} %copy-done.1, bf16[2,2,2,64,256]{4,3,2,1,0:T(8,128)(2,1)S(1)} %copy-done.6, bf16[4,8,64,128]{3,2,1,0:T(8,128)(2,1)S(1)} %get-tuple-element.8.second), custom_call_target="tpu_custom_call" | custom-call | tf_op jit(solution)/shard_map/coarse_level/pallas_call | solution.py:386
  83.7 9.3 %halo2.1.joined = bf16[6,10,64,128]{3,2,1,0:T(8,128)(2,1)S(1)} custom-call(bf16[4,8,64,128]{3,2,1,0:T(8,128)(2,1)S(1)} %coarse_level.1.block), custom_call_target="tpu_custom_call" | custom-call | tf_op jit(solution)/shard_map/halo2/pallas_call | solution.py:85
  93.1 0.0 copy-done.12
  93.1 0.0 copy-done.5
  93.1 3.7 %merge_level.1 = f32[3,4,8,128]{3,2,1,0:T(8,128)} custom-call(bf16[6,10,64,128]{3,2,1,0:T(8,128)(2,1)S(1)} %halo2.1.joined, bf16[3,3,64,192]{3,2,1,0:T(8,128)(2,1)S(1)} %copy-done.5, bf16[16,64]{1,0:T(8,128)(2,1)S(1)} %pad.9.head), custom_call_target="tpu_custom_call" | custom-call | tf_op jit(solution)/shard_map/merge_level/pallas_call | solution.py:416
  (1 shorter events, 0.0 us)
Async XLA Ops:
  0.7 0.8 copy-start.8
  1.5 0.7 copy-start.9
  2.2 0.7 copy-start.10
  2.9 0.7 copy-start.11
  3.6 75.5 %copy-start.1 = (bf16[3,3,256,768]{3,2,1,0:T(8,128)(2,1)S(1)}, bf16[3,3,256,768]{3,2,1,0:T(8,128)(2,1)}, u32[]{:S(2)}) copy-start(bf16[3,3,256,768]{3,2,1,0:T(8,128)(2,1)} %weight.2) | copy-start | bytes 10616836
  17.2 1.2 %copy-start = (bf16[8,4,6,32,128]{4,3,2,1,0:T(8,128)(2,1)}, bf16[8,4,6,32,128]{4,3,2,1,0:T(8,128)(2,1)S(1)}, u32[]{:S(2)}) copy-start(bf16[8,4,6,32,128]{4,3,2,1,0:T(8,128)(2,1)S(1)} %deposit.1) | copy-start | bytes 4718596
  58.2 1.0 %copy-start.2 = (f32[8,12,8,128]{3,2,1,0:T(8,128)S(1)}, f32[8,12,8,128]{3,2,1,0:T(8,128)}, u32[]{:S(2)}) copy-start(f32[8,12,8,128]{3,2,1,0:T(8,128)} %reduce_field.1.grid) | copy-start | bytes 1179652
  59.2 0.9 copy-start.3
  60.2 1.0 copy-start.4
  61.1 0.8 copy-start.7
  79.1 1.0 copy-start.6
  80.1 13.0 %copy-start.12 = (bf16[3,64]{1,0:T(4,128)(2,1)S(1)}, bf16[3,64]{1,0:T(4,128)(2,1)}, u32[]{:S(2)}) copy-start(bf16[3,64]{1,0:T(4,128)(2,1)} %param.23) | copy-start | bytes 1156
  80.1 13.0 %copy-start.5 = (bf16[3,3,64,192]{3,2,1,0:T(8,128)(2,1)S(1)}, bf16[3,3,64,192]{3,2,1,0:T(8,128)(2,1)}, u32[]{:S(2)}) copy-start(bf16[3,3,64,192]{3,2,1,0:T(8,128)(2,1)} %weight.3) | copy-start | bytes 663556

commit v3 on v2

--- a/solution.py
+++ b/solution.py
@@ -99,99 +99,89 @@
 
 def reduce_kernel(bits, field, padded, *scratch):
     tiles = lax.axis_size("tile")
+    attrs = field.shape[0]
     slab, tile = lax.axis_index("slab"), lax.axis_index("tile")
-    half = tiles // 2
     mine = [slab // 2**b % 2 for b in range(bits)]
     partner = [(slab + 2**b * (1 - 2 * mine[b]), tile) for b in range(bits)]
     ahead = [(slab, lax.rem(tile + d, tiles)) for d in range(1, tiles)]
     greet(partner + ahead + [neighbour(dz, dy) for dz, dy in SIDES])
-    gets, sums = scratch[: 2 * bits], scratch[2 * bits : 4 * bits]
-    last, block, send, recv, send_z, recv_z, send_h, recv_h, whole = scratch[4 * bits :]
-
-    def start(source, target, sem, device):
+    gets, sums = scratch[:bits], scratch[bits : 2 * bits]
+    last, block, send, recv, send_z, recv_z, send_h, recv_h = scratch[2 * bits :]
+    orders = [[0] + list(range(1, bits)), [0] + list(range(bits - 1, 0, -1))]
+
+    def part(c, stage, side):
+        order = orders[c % 2]
+        rest = [b for b in range(bits - 1, -1, -1) if b not in order[:stage]]
+        b = order[stage]
+        source = field if stage == 0 else sums[stage - 1]
+        which = mine[b] if side == 0 else 1 - mine[b]
+        return source, (c,) + (slice(None),) * rest.index(b) + (which,)
+
+    def push(c, stage):
+        source, at = part(c, stage, 1)
         copy = pltpu.make_async_remote_copy(
-            src_ref=source,
-            dst_ref=target,
-            send_sem=send.at[sem],
-            recv_sem=recv.at[sem],
-            device_id=device,
+            src_ref=source.at[at],
+            dst_ref=gets[stage].at[c],
+            send_sem=send.at[stage, c],
+            recv_sem=recv.at[stage, c],
+            device_id=partner[orders[c % 2][stage]],
             device_id_type=MESH,
         )
         copy.start()
         return copy
 
-    orders = [[0] + list(range(1, bits)), [0] + list(range(bits - 1, 0, -1))]
-    left = [list(range(bits - 1, -1, -1)) for _ in range(2)]
-    here = [None, None]
+    def deal(c):
+        copies = []
+        for d in range(1, tiles):
+            copy = pltpu.make_async_remote_copy(
+                src_ref=sums[bits - 1].at[c, lax.rem(tile + d, tiles)],
+                dst_ref=last.at[c, d - 1],
+                send_sem=send_z.at[c, d - 1],
+                recv_sem=recv_z.at[c, d - 1],
+                device_id=ahead[d - 1],
+                device_id_type=MESH,
+            )
+            copy.start()
+            copies.append(copy)
+        return copies
+
+    flying = [push(c, 0) for c in range(attrs)]
     for stage in range(bits):
-        copies = []
-        for h in range(2):
-            b = orders[h][stage]
-            at = (slice(None),) * left[h].index(b)
-            parts = pl.ds(h * half, half)
-            if stage == 0:
-                away = field.at[at + (1 - mine[b], parts)]
-            else:
-                away = here[h].at[at + (1 - mine[b],)]
-            copies.append(start(away, gets[2 * stage + h], 2 * stage + h, partner[b]))
-        for h in range(2):
-            b = orders[h][stage]
-            at = (slice(None),) * left[h].index(b)
-            parts = pl.ds(h * half, half)
-            copies[h].wait()
-            if stage == 0:
-                own = field[at + (mine[b], parts)]
-            else:
-                own = here[h][at + (mine[b],)]
-            total = own.astype(F32) + gets[2 * stage + h][...].astype(F32)
-            sums[2 * stage + h][...] = total.astype(BF16)
-            here[h] = sums[2 * stage + h]
-            left[h].remove(b)
-    whole[pl.ds(0, half)] = here[0][...]
-    whole[pl.ds(half, half)] = here[1][...]
-    copies = []
-    for d in range(1, tiles):
-        copy = pltpu.make_async_remote_copy(
-            src_ref=whole.at[lax.rem(tile + d, tiles)],
-            dst_ref=last.at[d - 1],
-            send_sem=send_z.at[d - 1],
-            recv_sem=recv_z.at[d - 1],
-            device_id=ahead[d - 1],
-            device_id_type=MESH,
-        )
-        copy.start()
-        copies.append(copy)
-    total = whole[tile].astype(F32)
-    for d in range(1, tiles):
-        copies[d - 1].wait()
-        total = total + last[d - 1].astype(F32)
-    total = total.astype(BF16).astype(F32)
+        for c in range(attrs):
+            flying[c].wait()
+            source, at = part(c, stage, 0)
+            total = source[at].astype(F32) + gets[stage][c].astype(F32)
+            sums[stage][c] = total.astype(BF16)
+            flying[c] = push(c, stage + 1) if stage < bits - 1 else deal(c)
     block[...] = jnp.zeros_like(block)
-    for c in range(total.shape[0]):
+    for c in range(attrs):
+        total = sums[bits - 1][c, tile].astype(F32)
+        for d in range(1, tiles):
+            flying[c][d - 1].wait()
+            total = total + last[c, d - 1].astype(F32)
+        total = total.astype(BF16).astype(F32)
         for z in range(CZ):
-            block[z, :, c, :] = total[c, z * YT : (z + 1) * YT]
+            block[z, :, c, :] = total[z * YT : (z + 1) * YT]
     exchange(block, padded, 2, send_h, recv_h)
 
 
 def reduce_field(field):
-    slabs, tiles, attrs, size, lanes = field.shape
+    attrs, slabs, tiles, size, lanes = field.shape
     bits = slabs.bit_length() - 1
-    half = tiles // 2
-    parts = []
-    for stage in range(bits):
-        shape = (2,) * (bits - 1 - stage) + (half, attrs, size, lanes)
-        parts += [pltpu.VMEM(shape, BF16)] * 2
+    parts = [
+        pltpu.VMEM((attrs,) + (2,) * (bits - 1 - stage) + (tiles, size, lanes), BF16)
+        for stage in range(bits)
+    ]
     scratch = parts + parts
     scratch += [
-        pltpu.VMEM((tiles - 1, attrs, size, lanes), BF16),
+        pltpu.VMEM((attrs, tiles - 1, size, lanes), BF16),
         pltpu.VMEM((CZ, YT, 8, lanes), F32),
-        pltpu.SemaphoreType.DMA((2 * bits,)),
-        pltpu.SemaphoreType.DMA((2 * bits,)),
-        pltpu.SemaphoreType.DMA((tiles - 1,)),
-        pltpu.SemaphoreType.DMA((tiles - 1,)),
+        pltpu.SemaphoreType.DMA((bits, attrs)),
+        pltpu.SemaphoreType.DMA((bits, attrs)),
+        pltpu.SemaphoreType.DMA((attrs, tiles - 1)),
+        pltpu.SemaphoreType.DMA((attrs, tiles - 1)),
         pltpu.SemaphoreType.DMA((8,)),
         pltpu.SemaphoreType.DMA((8,)),
-        pltpu.VMEM((tiles, attrs, size, lanes), BF16),
     ]
     return pl.pallas_call(
         functools.partial(reduce_kernel, bits),
@@ -203,7 +193,7 @@
             collective_id=0, has_side_effects=True, vmem_limit_bytes=56 << 20
         ),
         name="reduce_field",
-    )(field.reshape((2,) * bits + field.shape[1:]))
+    )(field.reshape((attrs,) + (2,) * bits + field.shape[2:]))
 
 
 def spread(values):
@@ -237,8 +227,28 @@
     return lax.broadcasted_iota(jnp.int32, (rows, 128), 1)
 
 
-def fine_kernel(grid, lift, fine, down, second, lowered, wide, stack, acc):
+def place(rows, columns, target_of):
+    source = lax.broadcasted_iota(jnp.int32, (rows, columns), 0)
+    target = lax.broadcasted_iota(jnp.int32, (rows, columns), 1)
+    return jnp.where(target == target_of(source), 1.0, 0.0).astype(BF16)
+
+
+def fine_kernel(grid, lift_raw, fine, down_raw, second, lowered, wide, stack, acc, lift, down):
     planes, rows = grid.shape[0] - 2, grid.shape[1] - 2
+    taps = lift_raw.shape[3]
+    each = taps // 3
+    total = None
+    for n in range(9):
+        spots = place(taps, 216, lambda i: n * 24 + i // each * 8 + i % each)
+        term = dot(lift_raw[n // 3, n % 3], spots)
+        total = term if total is None else total + term
+    lift[...] = total.astype(BF16)
+    depth = down_raw.shape[2]
+    total = None
+    for n in range(4):
+        term = dot(down_raw[n], place(depth, 4 * depth, lambda i: n * depth + i))
+        total = term if total is None else total + term
+    down[...] = total.astype(BF16)
     for z in range(planes + 2):
         block = grid[z]
         wide[z, :, 0:8] = pltpu.roll(block, 1, 2)
@@ -297,10 +307,7 @@
 def fine_level(grid, lift, fine, down):
     outs, chans = fine.shape[2], down.shape[3]
     planes, rows = grid.shape[0] - 2, grid.shape[1] - 2
-    wide = lift.reshape(3, 3, outs, 3, -1)
-    wide = jnp.pad(wide, ((0, 0),) * 4 + ((0, 8 - wide.shape[4]),))
-    wide = wide.transpose(2, 0, 1, 3, 4).reshape(outs, -1)
-    low = down.transpose(2, 3, 0, 1, 4).reshape(2 * chans, 4 * outs)
+    low = down.reshape(4, 2 * chans, outs)
     return pl.pallas_call(
         fine_kernel,
         out_shape=(
@@ -311,10 +318,12 @@
             pltpu.VMEM((planes + 2, rows + 2, 24, NX), F32),
             pltpu.VMEM((planes, rows, 3 * outs, NX), BF16),
             pltpu.VMEM((CZ, YT // 2, outs, 2 * NX), F32),
+            pltpu.VMEM((outs, 216), BF16),
+            pltpu.VMEM((2 * chans, 4 * outs), BF16),
         ],
         compiler_params=pltpu.CompilerParams(vmem_limit_bytes=48 << 20),
         name="fine_level",
-    )(grid, wide, fine, low)
+    )(grid, lift, fine, low)
 
 
 def coarse_kernel(low, weight, up, second, joined, acc):
@@ -412,7 +421,6 @@
 def merge_level(joined, weight, head):
     planes, rows, chans, lanes = joined.shape
     final = head.shape[0]
-    padded = jnp.pad(head, ((0, 16 - final), (0, 0)))
     return pl.pallas_call(
         merge_kernel,
         out_shape=jax.ShapeDtypeStruct((final, planes - 2, rows - 2, lanes), F32),
@@ -422,10 +430,10 @@
         ],
         compiler_params=pltpu.CompilerParams(vmem_limit_bytes=48 << 20),
         name="merge_level",
-    )(joined, weight, padded)
-
-
-GROUP = 4
+    )(joined, weight, head)
+
+
+GROUP = 8
 CHUNK = 512
 
 
@@ -499,7 +507,7 @@
         for t in range(tiles):
             k = (s * tiles + t) * size
             for c in range(attrs):
-                out_ref[s, t, c] = acc[k : k + size, c * NX : (c + 1) * NX].astype(jnp.bfloat16)
+                out_ref[c, s, t] = acc[k : k + size, c * NX : (c + 1) * NX].astype(jnp.bfloat16)
 
 
 def deposit(features, destination, cell_index, offset_code, live_count, slabs, tiles):
@@ -516,13 +524,13 @@
             whole((1, rows)),
             pl.BlockSpec(memory_space=pltpu.SMEM),
         ],
-        out_specs=pl.BlockSpec((GROUP, tiles, attrs, size, NX), lambda g: (g, 0, 0, 0, 0)),
-        out_shape=jax.ShapeDtypeStruct((slabs, tiles, attrs, size, NX), jnp.bfloat16),
+        out_specs=pl.BlockSpec((attrs, GROUP, tiles, size, NX), lambda g: (0, g, 0, 0, 0)),
+        out_shape=jax.ShapeDtypeStruct((attrs, slabs, tiles, size, NX), jnp.bfloat16),
         scratch_shapes=[
             pltpu.VMEM((attrs * NX, rows), jnp.bfloat16),
             pltpu.VMEM((GROUP * tiles * size, attrs * NX), jnp.float32),
         ],
-        compiler_params=pltpu.CompilerParams(vmem_limit_bytes=48 << 20),
+        compiler_params=pltpu.CompilerParams(vmem_limit_bytes=60 << 20),
         name="deposit",
     )(
         features,

time: 97.6 us -> 86.4 us (0.89)
  local copies, waits for them, and re-layouts: 17.3 us -> 8.44 us
  Pallas kernels: 78.7 us -> 76.7 us
    reshape x4 -> x0, local copies, waits for them, and re-layouts: 7.1 us -> none  [the longest x2 4.12 us: fine_level(): low = down.transpose(2, 3, 0, 1, 4).reshape(2 * chans, 4 * outs)]
    pallas_call x1, Pallas kernels: 31.3 us -> 28.3 us  [reduce_field(): pl.pallas_call(functools.partial(reduce_kernel, bits), in_specs=[pl.Block...]
    pad x2 -> x0, local copies, waits for them, and re-layouts: 1.47 us -> none  [the longest x1 1.46 us: fine_level(): wide = jnp.pad(wide, ((0, 0),) * 4 + ((0, 8 - wide.shape[4]),))]
    unnamed x26 -> x18, local copies, waits for them, and re-layouts: 8.76 us -> 8.44 us
where the time goes in v3:
time: 86.4 us; the launch traced here: 86 us
  Pallas kernels  76.7 us (89%)
  local copies, waits for them, and re-layouts  8.44 us (10%)
  between operations  0.88 us (1%)
    pallas_call x1, Pallas kernels, reduce_field(): pl.pallas_call(functools.partial(reduce_kernel, bits), in_specs=[pl.Block...  28.3 us
    pallas_call x2, Pallas kernels, with_halo(): pl.pallas_call(functools.partial(halo_kernel, width), in_specs=[pl.BlockS...  21.8 us
    pallas_call x1, Pallas kernels, deposit(): pl.pallas_call(functools.partial(deposit_kernel, slabs, tiles), grid=(sla...  14 us
    unnamed x18, local copies, waits for them, and re-layouts  8.44 us
    pallas_call x1, Pallas kernels, fine_level(): pl.pallas_call(fine_kernel, out_shape=(jax.ShapeDtypeStruct((CZ, YT, outs...  5.16 us
    pallas_call x1, Pallas kernels, merge_level(): pl.pallas_call(merge_kernel, out_shape=jax.ShapeDtypeStruct((final, plane...  3.68 us
    pallas_call x1, Pallas kernels, coarse_level(): pl.pallas_call(coarse_kernel, out_shape=jax.ShapeDtypeStruct(second.shape...  3.63 us

profile of v3, /device:TPU:0, one launch (start us, length us, event | category | flops | bytes accessed | tf_op | source)
XLA Modules:
  0.0 86.0 jit_solution(14382463378226900687)
XLA Ops:
  0.0 0.0 copy-start
  0.8 14.0 %deposit.1 = bf16[6,8,4,32,128]{4,3,2,1,0:T(8,128)(2,1)} custom-call(bf16[6,4096]{1,0:T(8,128)(2,1)} %feat_ref.1, s32[1,4096]{1,0:T(1,128)} %bitcast.7, s32[1,4096]{1,0:T(1,128)} %bitcast.8, s32[1,4096]{1,0:T(1,128)} %bitcast.9, s32[1]{0:T(128)S(6)} %copy.15.live_ref), custom_call_target="tpu_custom_call" | custom-call | tf_op jit(solution)/shard_map/deposit/pallas_call | solution.py:517
  14.8 28.3 %reduce_field.1.grid = f32[8,12,8,128]{3,2,1,0:T(8,128)} custom-call(bf16[6,2,2,2,4,32,128]{6,5,4,3,2,1,0:T(8,128)(2,1)} %bitcast.6), custom_call_target="tpu_custom_call" | custom-call | tf_op jit(solution)/shard_map/reduce_field/pallas_call | solution.py:186
  43.2 2.0 %copy.13 = bf16[2,2,2,256,64]{4,3,2,1,0:T(8,128)(2,1)} copy(bf16[2,2,2,256,64]{3,4,2,1,0:T(8,128)(2,1)} %param.19) | data formatting | bytes 524288 | tf_op args[7]
  45.1 1.6 %copy.14.lift_raw = bf16[3,3,64,18]{3,2,1,0:T(8,128)(2,1)} copy(bf16[3,3,64,18]{2,3,1,0:T(8,128)(2,1)} %param.17) | data formatting | bytes 41472 | tf_op args[5]
  46.7 0.0 copy-start.1
  46.7 1.0 %copy-done.1 = bf16[2,2,2,256,64]{4,3,2,1,0:T(8,128)(2,1)S(1)} copy-done((bf16[2,2,2,256,64]{4,3,2,1,0:T(8,128)(2,1)S(1)}, bf16[2,2,2,256,64]{4,3,2,1,0:T(8,128)(2,1)}, u32[]{:S(2)}) %copy-start.1) | copy-done | bytes 262168
  47.8 0.0 copy-start.2
  47.8 1.0 %copy-done.2 = f32[8,12,8,128]{3,2,1,0:T(8,128)S(1)} copy-done((f32[8,12,8,128]{3,2,1,0:T(8,128)S(1)}, f32[8,12,8,128]{3,2,1,0:T(8,128)}, u32[]{:S(2)}) %copy-start.2) | copy-done | bytes 393240
  48.8 0.0 copy-start.3
  48.8 0.9 %copy-done.3 = bf16[3,3,64,18]{3,2,1,0:T(8,128)(2,1)S(1)} copy-done((bf16[3,3,64,18]{3,2,1,0:T(8,128)(2,1)S(1)}, bf16[3,3,64,18]{3,2,1,0:T(8,128)(2,1)}, u32[]{:S(2)}) %copy-start.3) | copy-done | bytes 20760
  49.7 0.0 copy-start.4
  49.7 1.0 %copy-done.4 = bf16[3,3,64,192]{3,2,1,0:T(8,128)(2,1)S(1)} copy-done((bf16[3,3,64,192]{3,2,1,0:T(8,128)(2,1)S(1)}, bf16[3,3,64,192]{3,2,1,0:T(8,128)(2,1)}, u32[]{:S(2)}) %copy-start.4) | copy-done | bytes 221208
  50.6 5.2 %fine_level.1 = (bf16[4,8,64,128]{3,2,1,0:T(8,128)(2,1)S(1)}, bf16[2,4,128,128]{3,2,1,0:T(8,128)(2,1)S(1)}) custom-call(f32[8,12,8,128]{3,2,1,0:T(8,128)S(1)} %copy-done.2, bf16[3,3,64,18]{3,2,1,0:T(8,128)(2,1)S(1)} %copy-done.3, bf16[3,3,64,192]{3,2,1,0:T(8,128)(2,1)S(1)} %copy-done.4, bf16[4,512,64]{2,1,0:T(8,128)(2,1)S(1)} %bitcast.5), custom_call_target="tpu_custom_call" | custom-call | tf_op jit(solution)/shard_map/fine_level/pallas_call | solution.py:311
  55.8 12.2 %halo1.1.low = bf16[4,6,128,128]{3,2,1,0:T(8,128)(2,1)S(1)} custom-call(bf16[2,4,128,128]{3,2,1,0:T(8,128)(2,1)S(1)} %get-tuple-element.7.block), custom_call_target="tpu_custom_call" | custom-call | tf_op jit(solution)/shard_map/halo1/pallas_call | solution.py:85
  68.0 0.0 copy-done
  68.1 0.0 copy-start.6
  68.1 0.9 %copy-done.6 = bf16[2,2,2,64,256]{4,3,2,1,0:T(8,128)(2,1)S(1)} copy-done((bf16[2,2,2,64,256]{4,3,2,1,0:T(8,128)(2,1)S(1)}, bf16[2,2,2,64,256]{4,3,2,1,0:T(8,128)(2,1)}, u32[]{:S(2)}) %copy-start.6) | copy-done | bytes 262168
  69.0 0.0 copy-start.5
  69.0 0.0 copy-start.7
  69.0 3.6 %coarse_level.1.block = bf16[4,8,64,128]{3,2,1,0:T(8,128)(2,1)S(1)} custom-call(bf16[4,6,128,128]{3,2,1,0:T(8,128)(2,1)S(1)} %halo1.1.low, bf16[3,3,256,768]{3,2,1,0:T(8,128)(2,1)S(1)} %copy-done, bf16[2,2,2,64,256]{4,3,2,1,0:T(8,128)(2,1)S(1)} %copy-done.6, bf16[4,8,64,128]{3,2,1,0:T(8,128)(2,1)S(1)} %get-tuple-element.8.second), custom_call_target="tpu_custom_call" | custom-call | tf_op jit(solution)/shard_map/coarse_level/pallas_call | solution.py:395
  72.7 9.6 %halo2.1.joined = bf16[6,10,64,128]{3,2,1,0:T(8,128)(2,1)S(1)} custom-call(bf16[4,8,64,128]{3,2,1,0:T(8,128)(2,1)S(1)} %coarse_level.1.block), custom_call_target="tpu_custom_call" | custom-call | tf_op jit(solution)/shard_map/halo2/pallas_call | solution.py:85
  82.3 0.0 copy-done.5
  82.3 0.0 copy-done.7
  82.3 3.7 %merge_level.1 = f32[3,4,8,128]{3,2,1,0:T(8,128)} custom-call(bf16[6,10,64,128]{3,2,1,0:T(8,128)(2,1)S(1)} %halo2.1.joined, bf16[3,3,64,192]{3,2,1,0:T(8,128)(2,1)S(1)} %copy-done.5, bf16[3,64]{1,0:T(4,128)(2,1)S(1)} %copy-done.7), custom_call_target="tpu_custom_call" | custom-call | tf_op jit(solution)/shard_map/merge_level/pallas_call | solution.py:424
Async XLA Ops:
  0.0 68.1 %copy-start = (bf16[3,3,256,768]{3,2,1,0:T(8,128)(2,1)S(1)}, bf16[3,3,256,768]{3,2,1,0:T(8,128)(2,1)}, u32[]{:S(2)}) copy-start(bf16[3,3,256,768]{3,2,1,0:T(8,128)(2,1)} %weight.2) | copy-start | bytes 10616836
  46.7 1.0 %copy-start.1 = (bf16[2,2,2,256,64]{4,3,2,1,0:T(8,128)(2,1)S(1)}, bf16[2,2,2,256,64]{4,3,2,1,0:T(8,128)(2,1)}, u32[]{:S(2)}) copy-start(bf16[2,2,2,256,64]{4,3,2,1,0:T(8,128)(2,1)} %copy.13) | copy-start | bytes 786436
  47.8 1.0 %copy-start.2 = (f32[8,12,8,128]{3,2,1,0:T(8,128)S(1)}, f32[8,12,8,128]{3,2,1,0:T(8,128)}, u32[]{:S(2)}) copy-start(f32[8,12,8,128]{3,2,1,0:T(8,128)} %reduce_field.1.grid) | copy-start | bytes 1179652
  48.8 0.9 %copy-start.3 = (bf16[3,3,64,18]{3,2,1,0:T(8,128)(2,1)S(1)}, bf16[3,3,64,18]{3,2,1,0:T(8,128)(2,1)}, u32[]{:S(2)}) copy-start(bf16[3,3,64,18]{3,2,1,0:T(8,128)(2,1)} %copy.14.lift_raw) | copy-start | bytes 62212
  49.7 1.0 %copy-start.4 = (bf16[3,3,64,192]{3,2,1,0:T(8,128)(2,1)S(1)}, bf16[3,3,64,192]{3,2,1,0:T(8,128)(2,1)}, u32[]{:S(2)}) copy-start(bf16[3,3,64,192]{3,2,1,0:T(8,128)(2,1)} %fine.1) | copy-start | bytes 663556
  68.1 1.0 %copy-start.6 = (bf16[2,2,2,64,256]{4,3,2,1,0:T(8,128)(2,1)S(1)}, bf16[2,2,2,64,256]{4,3,2,1,0:T(8,128)(2,1)}, u32[]{:S(2)}) copy-start(bf16[2,2,2,64,256]{4,3,2,1,0:T(8,128)(2,1)} %up.1) | copy-start | bytes 786436
  69.0 13.3 %copy-start.5 = (bf16[3,3,64,192]{3,2,1,0:T(8,128)(2,1)S(1)}, bf16[3,3,64,192]{3,2,1,0:T(8,128)(2,1)}, u32[]{:S(2)}) copy-start(bf16[3,3,64,192]{3,2,1,0:T(8,128)(2,1)} %weight.3) | copy-start | bytes 663556
  69.0 13.3 %copy-start.7 = (bf16[3,64]{1,0:T(4,128)(2,1)S(1)}, bf16[3,64]{1,0:T(4,128)(2,1)}, u32[]{:S(2)}) copy-start(bf16[3,64]{1,0:T(4,128)(2,1)} %head.1) | copy-start | bytes 1156

commit v4 on v3

--- a/solution.py
+++ b/solution.py
@@ -75,36 +75,20 @@
         copy.wait()
 
 
-def halo_kernel(width, block, padded, send, recv):
-    greet([neighbour(dz, dy) for dz, dy in SIDES])
-    exchange(block, padded, width, send, recv)
-
-
-def with_halo(block, width, number):
-    planes, rows, depth, lanes = block.shape
-    return pl.pallas_call(
-        functools.partial(halo_kernel, width),
-        in_specs=[pl.BlockSpec(memory_space=pltpu.VMEM)],
-        out_specs=pl.BlockSpec(memory_space=pltpu.VMEM),
-        out_shape=jax.ShapeDtypeStruct(
-            (planes + 2 * width, rows + 2 * width, depth, lanes), block.dtype
-        ),
-        scratch_shapes=[pltpu.SemaphoreType.DMA((8,)), pltpu.SemaphoreType.DMA((8,))],
-        compiler_params=pltpu.CompilerParams(
-            collective_id=number, has_side_effects=True, vmem_limit_bytes=32 << 20
-        ),
-        name=f"halo{number}",
-    )(block)
-
-
-def reduce_kernel(bits, field, padded, *scratch):
+def meet(bits):
+    slab, tile, tiles = lax.axis_index("slab"), lax.axis_index("tile"), lax.axis_size("tile")
+    partner = [(slab + 2**b * (1 - 2 * (slab // 2**b % 2)), tile) for b in range(bits)]
+    ahead = [(slab, lax.rem(tile + d, tiles)) for d in range(1, tiles)]
+    greet(partner + ahead + [neighbour(dz, dy) for dz, dy in SIDES])
+
+
+def reduce_stage(bits, field, padded, *scratch):
     tiles = lax.axis_size("tile")
     attrs = field.shape[0]
     slab, tile = lax.axis_index("slab"), lax.axis_index("tile")
     mine = [slab // 2**b % 2 for b in range(bits)]
     partner = [(slab + 2**b * (1 - 2 * mine[b]), tile) for b in range(bits)]
     ahead = [(slab, lax.rem(tile + d, tiles)) for d in range(1, tiles)]
-    greet(partner + ahead + [neighbour(dz, dy) for dz, dy in SIDES])
     gets, sums = scratch[:bits], scratch[bits : 2 * bits]
     last, block, send, recv, send_z, recv_z, send_h, recv_h = scratch[2 * bits :]
     orders = [[0] + list(range(1, bits)), [0] + list(range(bits - 1, 0, -1))]
@@ -163,37 +147,6 @@
         for z in range(CZ):
             block[z, :, c, :] = total[z * YT : (z + 1) * YT]
     exchange(block, padded, 2, send_h, recv_h)
-
-
-def reduce_field(field):
-    attrs, slabs, tiles, size, lanes = field.shape
-    bits = slabs.bit_length() - 1
-    parts = [
-        pltpu.VMEM((attrs,) + (2,) * (bits - 1 - stage) + (tiles, size, lanes), BF16)
-        for stage in range(bits)
-    ]
-    scratch = parts + parts
-    scratch += [
-        pltpu.VMEM((attrs, tiles - 1, size, lanes), BF16),
-        pltpu.VMEM((CZ, YT, 8, lanes), F32),
-        pltpu.SemaphoreType.DMA((bits, attrs)),
-        pltpu.SemaphoreType.DMA((bits, attrs)),
-        pltpu.SemaphoreType.DMA((attrs, tiles - 1)),
-        pltpu.SemaphoreType.DMA((attrs, tiles - 1)),
-        pltpu.SemaphoreType.DMA((8,)),
-        pltpu.SemaphoreType.DMA((8,)),
-    ]
-    return pl.pallas_call(
-        functools.partial(reduce_kernel, bits),
-        in_specs=[pl.BlockSpec(memory_space=pltpu.VMEM)],
-        out_specs=pl.BlockSpec(memory_space=pltpu.VMEM),
-        out_shape=jax.ShapeDtypeStruct((CZ + 4, YT + 4, 8, lanes), F32),
-        scratch_shapes=scratch,
-        compiler_params=pltpu.CompilerParams(
-            collective_id=0, has_side_effects=True, vmem_limit_bytes=56 << 20
-        ),
-        name="reduce_field",
-    )(field.reshape((attrs,) + (2,) * bits + field.shape[2:]))
 
 
 def spread(values):
@@ -227,6 +180,10 @@
     return lax.broadcasted_iota(jnp.int32, (rows, 128), 1)
 
 
+def cross(left, right):
+    return lax.dot_general(left, right, (((0,), (0,)), ((), ())), preferred_element_type=F32)
+
+
 def place(rows, columns, target_of):
     source = lax.broadcasted_iota(jnp.int32, (rows, columns), 0)
     target = lax.broadcasted_iota(jnp.int32, (rows, columns), 1)
@@ -235,20 +192,22 @@
 
 def fine_kernel(grid, lift_raw, fine, down_raw, second, lowered, wide, stack, acc, lift, down):
     planes, rows = grid.shape[0] - 2, grid.shape[1] - 2
-    taps = lift_raw.shape[3]
+    taps = lift_raw.shape[2]
     each = taps // 3
     total = None
     for n in range(9):
         spots = place(taps, 216, lambda i: n * 24 + i // each * 8 + i % each)
-        term = dot(lift_raw[n // 3, n % 3], spots)
+        term = cross(lift_raw[n // 3, n % 3], spots)
         total = term if total is None else total + term
     lift[...] = total.astype(BF16)
-    depth = down_raw.shape[2]
-    total = None
-    for n in range(4):
-        term = dot(down_raw[n], place(depth, 4 * depth, lambda i: n * depth + i))
-        total = term if total is None else total + term
-    down[...] = total.astype(BF16)
+    depth, tall = down_raw.shape[3:]
+    for k in range(2):
+        total = None
+        for n in range(4):
+            spots = place(depth, 4 * depth, lambda i: n * depth + i)
+            term = cross(down_raw[n // 2, n % 2, k], spots)
+            total = term if total is None else total + term
+        down[k * tall : (k + 1) * tall] = total.astype(BF16)
     for z in range(planes + 2):
         block = grid[z]
         wide[z, :, 0:8] = pltpu.roll(block, 1, 2)
@@ -302,28 +261,6 @@
                     jnp.where(lane < half, q01, q10), half, 1
                 )
                 lowered[z, 2 * j + s] = act(row).astype(BF16)
-
-
-def fine_level(grid, lift, fine, down):
-    outs, chans = fine.shape[2], down.shape[3]
-    planes, rows = grid.shape[0] - 2, grid.shape[1] - 2
-    low = down.reshape(4, 2 * chans, outs)
-    return pl.pallas_call(
-        fine_kernel,
-        out_shape=(
-            jax.ShapeDtypeStruct((CZ, YT, outs, NX), BF16),
-            jax.ShapeDtypeStruct((CZ // 2, YT // 2, chans // 2, NX), BF16),
-        ),
-        scratch_shapes=[
-            pltpu.VMEM((planes + 2, rows + 2, 24, NX), F32),
-            pltpu.VMEM((planes, rows, 3 * outs, NX), BF16),
-            pltpu.VMEM((CZ, YT // 2, outs, 2 * NX), F32),
-            pltpu.VMEM((outs, 216), BF16),
-            pltpu.VMEM((2 * chans, 4 * outs), BF16),
-        ],
-        compiler_params=pltpu.CompilerParams(vmem_limit_bytes=48 << 20),
-        name="fine_level",
-    )(grid, lift, fine, low)
 
 
 def coarse_kernel(low, weight, up, second, joined, acc):
@@ -390,15 +327,82 @@
                         )
 
 
-def coarse_level(low, weight, up, second):
-    chans = weight.shape[2]
+def middle_kernel(bits, count, field, lift_raw, fine, down_raw, coarse_far, up, out, *scratch):
+    first, (grid, second, lowered, low, joined, wide, stack, acc, lift, down) = (
+        scratch[:count],
+        scratch[count : count + 10],
+    )
+    total, coarse, send_a, recv_a, send_b, recv_b, fetched = scratch[count + 10 :]
+    fetch = pltpu.make_async_copy(coarse_far, coarse, fetched)
+    fetch.start()
+    meet(bits)
+    reduce_stage(bits, field, grid, *first)
+    fine_kernel(grid, lift_raw, fine, down_raw, second, lowered, wide, stack, acc, lift, down)
+    exchange(lowered, low, 1, send_a, recv_a)
+    fetch.wait()
+    coarse_kernel(low, coarse, up, second, joined, total)
+    exchange(joined, out, 1, send_b, recv_b)
+
+
+def middle(field, lift, fine, down, coarse, up):
+    attrs, slabs, tiles, size, lanes = field.shape
+    bits = slabs.bit_length() - 1
+    outs, chans = fine.shape[2], coarse.shape[2]
+    parts = [
+        pltpu.VMEM((attrs,) + (2,) * (bits - 1 - stage) + (tiles, size, lanes), BF16)
+        for stage in range(bits)
+    ]
+    eight = pltpu.SemaphoreType.DMA((8,))
+    first = parts + parts
+    first += [
+        pltpu.VMEM((attrs, tiles - 1, size, lanes), BF16),
+        pltpu.VMEM((CZ, YT, 8, lanes), F32),
+        pltpu.SemaphoreType.DMA((bits, attrs)),
+        pltpu.SemaphoreType.DMA((bits, attrs)),
+        pltpu.SemaphoreType.DMA((attrs, tiles - 1)),
+        pltpu.SemaphoreType.DMA((attrs, tiles - 1)),
+        eight,
+        eight,
+    ]
+    planes, rows = CZ + 2, YT + 2
+    rest = [
+        pltpu.VMEM((planes + 2, rows + 2, 8, lanes), F32),
+        pltpu.VMEM((CZ, YT, outs, lanes), BF16),
+        pltpu.VMEM((CZ // 2, YT // 2, chans // 2, lanes), BF16),
+        pltpu.VMEM((CZ // 2 + 2, YT // 2 + 2, chans // 2, lanes), BF16),
+        pltpu.VMEM((CZ, YT, outs, lanes), BF16),
+        pltpu.VMEM((planes + 2, rows + 2, 24, lanes), F32),
+        pltpu.VMEM((planes, rows, 3 * outs, lanes), BF16),
+        pltpu.VMEM((CZ, YT // 2, outs, 2 * lanes), F32),
+        pltpu.VMEM((outs, 216), BF16),
+        pltpu.VMEM((2 * chans, 4 * outs), BF16),
+        pltpu.VMEM((CZ // 2, 3, chans, 2 * lanes), F32),
+        pltpu.VMEM(coarse.shape, BF16),
+        eight,
+        eight,
+        eight,
+        eight,
+        pltpu.SemaphoreType.DMA,
+    ]
+    near = pl.BlockSpec(memory_space=pltpu.VMEM)
     return pl.pallas_call(
-        coarse_kernel,
-        out_shape=jax.ShapeDtypeStruct(second.shape, BF16),
-        scratch_shapes=[pltpu.VMEM((CZ // 2, 3, chans, 2 * NX), F32)],
-        compiler_params=pltpu.CompilerParams(vmem_limit_bytes=48 << 20),
-        name="coarse_level",
-    )(low, weight, up, second)
+        functools.partial(middle_kernel, bits, len(first)),
+        in_specs=[near, near, near, near, pl.BlockSpec(memory_space=pl.ANY), near],
+        out_specs=near,
+        out_shape=jax.ShapeDtypeStruct((planes, rows, outs, lanes), BF16),
+        scratch_shapes=first + rest,
+        compiler_params=pltpu.CompilerParams(
+            collective_id=0, has_side_effects=True, vmem_limit_bytes=56 << 20
+        ),
+        name="middle",
+    )(
+        field.reshape((attrs,) + (2,) * bits + field.shape[2:]),
+        lift.swapaxes(2, 3),
+        fine,
+        down.swapaxes(3, 4),
+        coarse,
+        up,
+    )
 
 
 def merge_kernel(joined, weight, head, out, stack, acc):
@@ -560,11 +564,7 @@
     field = deposit(
         particle_features, destination, cell_index, offset_code, live_count, slabs, tiles
     )
-    grid = reduce_field(field)
-    second, lowered = fine_level(grid, lift_weight, fine_weight, down_weight)
-    lowered = with_halo(lowered, 1, 1)
-    joined = coarse_level(lowered, coarse_weight, up_weight, second)
-    joined = with_halo(joined, 1, 2)
+    joined = middle(field, lift_weight, fine_weight, down_weight, coarse_weight, up_weight)
     return merge_level(joined, merge_weight, head_weight)
 
 

time: 86.4 us -> 72.6 us (0.84)
  local copies, waits for them, and re-layouts: 8.44 us -> 1.2 us
  Pallas kernels: 76.7 us -> 70.5 us
    unnamed x18 -> x6, local copies, waits for them, and re-layouts: 8.44 us -> 1.2 us
    pallas_call x5 -> x1, Pallas kernels: 58.9 us -> 52.9 us  [middle(): pl.pallas_call(functools.partial(middle_kernel, bits, len(first)), in_spe...]
where the time goes in v4:
time: 72.6 us; the launch traced here: 72.4 us
  Pallas kernels  70.5 us (97%)
  local copies, waits for them, and re-layouts  1.2 us (2%)
    pallas_call x1, Pallas kernels, middle(): pl.pallas_call(functools.partial(middle_kernel, bits, len(first)), in_spe...  52.9 us
    pallas_call x1, Pallas kernels, deposit(): pl.pallas_call(functools.partial(deposit_kernel, slabs, tiles), grid=(sla...  13.9 us
    pallas_call x1, Pallas kernels, merge_level(): pl.pallas_call(merge_kernel, out_shape=jax.ShapeDtypeStruct((final, plane...  3.67 us

profile of v4, /device:TPU:0, one launch (start us, length us, event | category | flops | bytes accessed | tf_op | source)
XLA Modules:
  0.0 72.4 jit_solution(8128465665954465984)
XLA Ops:
  0.7 13.9 %deposit.1 = bf16[6,8,4,32,128]{4,3,2,1,0:T(8,128)(2,1)} custom-call(bf16[6,4096]{1,0:T(8,128)(2,1)} %feat_ref.1, s32[1,4096]{1,0:T(1,128)} %bitcast.9, s32[1,4096]{1,0:T(1,128)} %bitcast.10, s32[1,4096]{1,0:T(1,128)} %bitcast.11, s32[1]{0:T(128)S(6)} %copy.13.live_ref), custom_call_target="tpu_custom_call" | custom-call | tf_op jit(solution)/shard_map/deposit/pallas_call | solution.py:521
  14.5 0.0 copy-start.1
  14.5 0.0 copy-start.2
  14.5 52.9 %middle.1.joined = bf16[6,10,64,128]{3,2,1,0:T(8,128)(2,1)} custom-call(bf16[6,2,2,2,4,32,128]{6,5,4,3,2,1,0:T(8,128)(2,1)} %bitcast.6, bf16[3,3,18,64]{3,2,1,0:T(8,128)(2,1)} %bitcast.8, bf16[3,3,64,192]{3,2,1,0:T(8,128)(2,1)} %fine.1, bf16[2,2,2,64,256]{4,3,2,1,0:T(8,128)(2,1)} %bitcast.7, bf16[3,3,256,768]{3,2,1,0:T(8,128)(2,1)} %coarse_far.1, ...), custom_call_target="tpu_custom_call" | custom-call | tf_op jit(solution)/shard_map/middle/pallas_call | solution.py:388
  67.5 0.0 copy-done.1
  67.5 0.0 copy-done.2
  67.5 0.0 copy-start
  67.5 1.2 %copy-done = bf16[6,10,64,128]{3,2,1,0:T(8,128)(2,1)S(1)} copy-done((bf16[6,10,64,128]{3,2,1,0:T(8,128)(2,1)S(1)}, bf16[6,10,64,128]{3,2,1,0:T(8,128)(2,1)}, u32[]{:S(2)}) %copy-start) | copy-done | bytes 983064
  68.7 3.7 %merge_level.1 = f32[3,4,8,128]{3,2,1,0:T(8,128)} custom-call(bf16[6,10,64,128]{3,2,1,0:T(8,128)(2,1)S(1)} %copy-done, bf16[3,3,64,192]{3,2,1,0:T(8,128)(2,1)S(1)} %copy-done.1, bf16[3,64]{1,0:T(4,128)(2,1)S(1)} %copy-done.2), custom_call_target="tpu_custom_call" | custom-call | tf_op jit(solution)/shard_map/merge_level/pallas_call | solution.py:428
Async XLA Ops:
  14.5 52.9 %copy-start.1 = (bf16[3,3,64,192]{3,2,1,0:T(8,128)(2,1)S(1)}, bf16[3,3,64,192]{3,2,1,0:T(8,128)(2,1)}, u32[]{:S(2)}) copy-start(bf16[3,3,64,192]{3,2,1,0:T(8,128)(2,1)} %weight.1) | copy-start | bytes 663556
  14.5 52.9 %copy-start.2 = (bf16[3,64]{1,0:T(4,128)(2,1)S(1)}, bf16[3,64]{1,0:T(4,128)(2,1)}, u32[]{:S(2)}) copy-start(bf16[3,64]{1,0:T(4,128)(2,1)} %head.1) | copy-start | bytes 1156
  67.5 1.2 %copy-start = (bf16[6,10,64,128]{3,2,1,0:T(8,128)(2,1)S(1)}, bf16[6,10,64,128]{3,2,1,0:T(8,128)(2,1)}, u32[]{:S(2)}) copy-start(bf16[6,10,64,128]{3,2,1,0:T(8,128)(2,1)} %middle.1.joined) | copy-start | bytes 2949124

commit v5 on v4

--- a/solution.py
+++ b/solution.py
@@ -75,6 +75,91 @@
         copy.wait()
 
 
+GROUP = 8
+CHUNK = 512
+DEEP = 1024
+
+
+def deposit_stage(bits, feat_ref, dest_ref, cell_ref, code_ref, live_ref, field, left, right, acc, ready):
+    attrs, rows = feat_ref.shape
+    slabs, tiles = 2**bits, field.shape[bits + 1]
+    ny = tiles * YT
+    nz = slabs * CZ
+    f32 = jnp.float32
+
+    def build(j, carry):
+        at = pl.ds(pl.multiple_of(j * CHUNK, CHUNK), CHUNK)
+        cells = cell_ref[:, at]
+        codes = code_ref[:, at]
+        lane = lax.broadcasted_iota(jnp.int32, (1, CHUNK), 1) + j * CHUNK
+        live = lane < live_ref[0]
+        feats = jnp.where(live, feat_ref[:, at].astype(f32), 0.0)
+        frac = (codes & 63).astype(f32) * (1.0 / 64.0)
+        col = cells & (NX - 1)
+        nxt = (col + 1) & (NX - 1)
+        xs = lax.broadcasted_iota(jnp.int32, (NX, CHUNK), 0)
+        wx = jnp.where(xs == col, 1.0 - frac, 0.0) + jnp.where(xs == nxt, frac, 0.0)
+        for c in range(attrs):
+            right[c * NX : (c + 1) * NX, at] = (wx * feats[c : c + 1, :]).astype(jnp.bfloat16)
+        return carry
+
+    lax.fori_loop(0, rows // CHUNK, build, 0)
+
+    def tall(j, group):
+        at = pl.ds(pl.multiple_of(j * CHUNK, CHUNK), CHUNK)
+        cells = cell_ref[:, at]
+        codes = code_ref[:, at]
+        fz = ((codes >> 12) & 63).astype(f32) * (1.0 / 64.0)
+        fy = ((codes >> 6) & 63).astype(f32) * (1.0 / 64.0)
+        row = cells // NX
+        y0 = row % ny
+        z0 = dest_ref[:, at] * CZ + row // ny
+        y1 = (y0 + 1) % ny
+        z1 = (z0 + 1) % nz
+        ys = lax.broadcasted_iota(jnp.int32, (ny, CHUNK), 0)
+        wy = jnp.where(ys == y0, 1.0 - fy, 0.0) + jnp.where(ys == y1, fy, 0.0)
+        zs = lax.broadcasted_iota(jnp.int32, (GROUP * CZ, CHUNK), 0) + group * GROUP * CZ
+        wz = jnp.where(zs == z0, 1.0 - fz, 0.0) + jnp.where(zs == z1, fz, 0.0)
+        pieces = []
+        for s in range(GROUP):
+            for t in range(tiles):
+                for z in range(CZ):
+                    k = s * CZ + z
+                    pieces.append(wz[k : k + 1, :] * wy[t * YT : (t + 1) * YT, :])
+        left[:, at] = jnp.concatenate(pieces, 0).astype(jnp.bfloat16)
+        return group
+
+    size = CZ * YT
+    groups = slabs // GROUP
+    for group in range(groups):
+        lax.fori_loop(0, rows // CHUNK, tall, group)
+        for n in range(attrs // 2):
+            acc[...] = jnp.zeros_like(acc)
+
+            def step(j, carry):
+                at = pl.ds(pl.multiple_of(j * DEEP, DEEP), DEEP)
+                acc[...] += lax.dot_general(
+                    left[:, at],
+                    right[2 * n * NX : (2 * n + 2) * NX, at],
+                    (((1,), (1,)), ((), ())),
+                    preferred_element_type=f32,
+                )
+                return carry
+
+            lax.fori_loop(0, rows // DEEP, step, 0)
+            for c in range(2):
+                for s in range(GROUP):
+                    slab = group * GROUP + s
+                    spot = tuple(slab // 2**b % 2 for b in range(bits - 1, -1, -1))
+                    for t in range(tiles):
+                        k = (s * tiles + t) * size
+                        field[(2 * n + c,) + spot + (t,)] = acc[
+                            k : k + size, c * NX : (c + 1) * NX
+                        ].astype(BF16)
+                if group == groups - 1:
+                    ready(2 * n + c)
+
+
 def meet(bits):
     slab, tile, tiles = lax.axis_index("slab"), lax.axis_index("tile"), lax.axis_size("tile")
     partner = [(slab + 2**b * (1 - 2 * (slab // 2**b % 2)), tile) for b in range(bits)]
@@ -82,7 +167,7 @@
     greet(partner + ahead + [neighbour(dz, dy) for dz, dy in SIDES])
 
 
-def reduce_stage(bits, field, padded, *scratch):
+def reduce_stage(bits, fill, field, padded, *scratch):
     tiles = lax.axis_size("tile")
     attrs = field.shape[0]
     slab, tile = lax.axis_index("slab"), lax.axis_index("tile")
@@ -129,7 +214,8 @@
             copies.append(copy)
         return copies
 
-    flying = [push(c, 0) for c in range(attrs)]
+    flying = []
+    fill(lambda c: flying.append(push(c, 0)))
     for stage in range(bits):
         for c in range(attrs):
             flying[c].wait()
@@ -327,7 +413,9 @@
                         )
 
 
-def middle_kernel(bits, count, field, lift_raw, fine, down_raw, coarse_far, up, out, *scratch):
+def middle_kernel(bits, count, feat, dest, cell, code, live, *rest):
+    lift_raw, fine, down_raw, coarse_far, up, out = rest[:6]
+    field, left, right, part, *scratch = rest[6:]
     first, (grid, second, lowered, low, joined, wide, stack, acc, lift, down) = (
         scratch[:count],
         scratch[count : count + 10],
@@ -336,7 +424,10 @@
     fetch = pltpu.make_async_copy(coarse_far, coarse, fetched)
     fetch.start()
     meet(bits)
-    reduce_stage(bits, field, grid, *first)
+    fill = functools.partial(
+        deposit_stage, bits, feat, dest, cell, code, live, field, left, right, part
+    )
+    reduce_stage(bits, fill, field, grid, *first)
     fine_kernel(grid, lift_raw, fine, down_raw, second, lowered, wide, stack, acc, lift, down)
     exchange(lowered, low, 1, send_a, recv_a)
     fetch.wait()
@@ -344,8 +435,10 @@
     exchange(joined, out, 1, send_b, recv_b)
 
 
-def middle(field, lift, fine, down, coarse, up):
-    attrs, slabs, tiles, size, lanes = field.shape
+def middle(features, destination, cells, codes, live, lift, fine, down, coarse, up):
+    attrs, total = features.shape
+    slabs, tiles = lax.axis_size("slab"), lax.axis_size("tile")
+    size, lanes = CZ * YT, NX
     bits = slabs.bit_length() - 1
     outs, chans = fine.shape[2], coarse.shape[2]
     parts = [
@@ -365,6 +458,13 @@
         eight,
     ]
     planes, rows = CZ + 2, YT + 2
+    tall = GROUP * tiles * size
+    early = [
+        pltpu.VMEM((attrs,) + (2,) * bits + (tiles, size, lanes), BF16),
+        pltpu.VMEM((tall, total), BF16),
+        pltpu.VMEM((attrs * lanes, total), BF16),
+        pltpu.VMEM((tall, 2 * lanes), F32),
+    ]
     rest = [
         pltpu.VMEM((planes + 2, rows + 2, 8, lanes), F32),
         pltpu.VMEM((CZ, YT, outs, lanes), BF16),
@@ -387,16 +487,23 @@
     near = pl.BlockSpec(memory_space=pltpu.VMEM)
     return pl.pallas_call(
         functools.partial(middle_kernel, bits, len(first)),
-        in_specs=[near, near, near, near, pl.BlockSpec(memory_space=pl.ANY), near],
+        in_specs=[near] * 4
+        + [pl.BlockSpec(memory_space=pltpu.SMEM)]
+        + [near] * 3
+        + [pl.BlockSpec(memory_space=pl.ANY), near],
         out_specs=near,
         out_shape=jax.ShapeDtypeStruct((planes, rows, outs, lanes), BF16),
-        scratch_shapes=first + rest,
+        scratch_shapes=early + first + rest,
         compiler_params=pltpu.CompilerParams(
-            collective_id=0, has_side_effects=True, vmem_limit_bytes=56 << 20
+            collective_id=0, has_side_effects=True, vmem_limit_bytes=60 << 20
         ),
         name="middle",
     )(
-        field.reshape((attrs,) + (2,) * bits + field.shape[2:]),
+        features,
+        destination.reshape(1, total),
+        cells.reshape(1, total),
+        codes.reshape(1, total),
+        live,
         lift.swapaxes(2, 3),
         fine,
         down.swapaxes(3, 4),
@@ -435,114 +542,6 @@
         compiler_params=pltpu.CompilerParams(vmem_limit_bytes=48 << 20),
         name="merge_level",
     )(joined, weight, head)
-
-
-GROUP = 8
-CHUNK = 512
-
-
-def deposit_kernel(slabs, tiles, feat_ref, dest_ref, cell_ref, code_ref, live_ref, out_ref, right, acc):
-    group = pl.program_id(0)
-    rows = feat_ref.shape[1]
-    attrs = feat_ref.shape[0]
-    ny = tiles * YT
-    nz = slabs * CZ
-    f32 = jnp.float32
-
-    @pl.when(group == 0)
-    def _():
-        def build(j, carry):
-            at = pl.ds(pl.multiple_of(j * CHUNK, CHUNK), CHUNK)
-            cells = cell_ref[:, at]
-            codes = code_ref[:, at]
-            lane = lax.broadcasted_iota(jnp.int32, (1, CHUNK), 1) + j * CHUNK
-            live = lane < live_ref[0]
-            feats = jnp.where(live, feat_ref[:, at].astype(f32), 0.0)
-            frac = (codes & 63).astype(f32) * (1.0 / 64.0)
-            col = cells & (NX - 1)
-            nxt = (col + 1) & (NX - 1)
-            xs = lax.broadcasted_iota(jnp.int32, (NX, CHUNK), 0)
-            wx = jnp.where(xs == col, 1.0 - frac, 0.0) + jnp.where(xs == nxt, frac, 0.0)
-            for c in range(attrs):
-                right[c * NX : (c + 1) * NX, at] = (wx * feats[c : c + 1, :]).astype(jnp.bfloat16)
-            return carry
-
-        lax.fori_loop(0, rows // CHUNK, build, 0)
-
-    def step(j, carry):
-        at = pl.ds(pl.multiple_of(j * CHUNK, CHUNK), CHUNK)
-        cells = cell_ref[:, at]
-        codes = code_ref[:, at]
-        fz = ((codes >> 12) & 63).astype(f32) * (1.0 / 64.0)
-        fy = ((codes >> 6) & 63).astype(f32) * (1.0 / 64.0)
-        row = cells // NX
-        y0 = row % ny
-        z0 = dest_ref[:, at] * CZ + row // ny
-        y1 = (y0 + 1) % ny
-        z1 = (z0 + 1) % nz
-        ys = lax.broadcasted_iota(jnp.int32, (ny, CHUNK), 0)
-        wy = jnp.where(ys == y0, 1.0 - fy, 0.0) + jnp.where(ys == y1, fy, 0.0)
-        zs = lax.broadcasted_iota(jnp.int32, (GROUP * CZ, CHUNK), 0) + group * GROUP * CZ
-        wz = jnp.where(zs == z0, 1.0 - fz, 0.0) + jnp.where(zs == z1, fz, 0.0)
-        pieces = []
-        for s in range(GROUP):
-            for t in range(tiles):
-                for z in range(CZ):
-                    k = s * CZ + z
-                    pieces.append(wz[k : k + 1, :] * wy[t * YT : (t + 1) * YT, :])
-        left = jnp.concatenate(pieces, 0).astype(jnp.bfloat16)
-        part = lax.dot_general(
-            left, right[:, at], (((1,), (1,)), ((), ())), preferred_element_type=f32
-        )
-
-        @pl.when(j == 0)
-        def _():
-            acc[...] = part
-
-        @pl.when(j > 0)
-        def _():
-            acc[...] += part
-
-        return carry
-
-    lax.fori_loop(0, rows // CHUNK, step, 0)
-    size = CZ * YT
-    for s in range(GROUP):
-        for t in range(tiles):
-            k = (s * tiles + t) * size
-            for c in range(attrs):
-                out_ref[c, s, t] = acc[k : k + size, c * NX : (c + 1) * NX].astype(jnp.bfloat16)
-
-
-def deposit(features, destination, cell_index, offset_code, live_count, slabs, tiles):
-    attrs, rows = features.shape
-    size = CZ * YT
-    whole = lambda shape: pl.BlockSpec(shape, lambda g: (0, 0))
-    return pl.pallas_call(
-        functools.partial(deposit_kernel, slabs, tiles),
-        grid=(slabs // GROUP,),
-        in_specs=[
-            whole((attrs, rows)),
-            whole((1, rows)),
-            whole((1, rows)),
-            whole((1, rows)),
-            pl.BlockSpec(memory_space=pltpu.SMEM),
-        ],
-        out_specs=pl.BlockSpec((attrs, GROUP, tiles, size, NX), lambda g: (0, g, 0, 0, 0)),
-        out_shape=jax.ShapeDtypeStruct((attrs, slabs, tiles, size, NX), jnp.bfloat16),
-        scratch_shapes=[
-            pltpu.VMEM((attrs * NX, rows), jnp.bfloat16),
-            pltpu.VMEM((GROUP * tiles * size, attrs * NX), jnp.float32),
-        ],
-        compiler_params=pltpu.CompilerParams(vmem_limit_bytes=60 << 20),
-        name="deposit",
-    )(
-        features,
-        destination.reshape(1, rows),
-        cell_index.reshape(1, rows),
-        offset_code.reshape(1, rows),
-        live_count,
-    )
 
 
 def body(
@@ -559,12 +558,18 @@
     merge_weight,
     head_weight,
 ):
-    slabs = lax.axis_size("slab")
-    tiles = lax.axis_size("tile")
-    field = deposit(
-        particle_features, destination, cell_index, offset_code, live_count, slabs, tiles
-    )
-    joined = middle(field, lift_weight, fine_weight, down_weight, coarse_weight, up_weight)
+    joined = middle(
+        particle_features,
+        destination,
+        cell_index,
+        offset_code,
+        live_count,
+        lift_weight,
+        fine_weight,
+        down_weight,
+        coarse_weight,
+        up_weight,
+    )
     return merge_level(joined, merge_weight, head_weight)
 
 

time: 72.6 us -> 68.6 us (0.945)
  Pallas kernels: 70.5 us -> 66.4 us
    pallas_call x1 -> x0, Pallas kernels: 13.9 us -> none  [deposit(): pl.pallas_call(functools.partial(deposit_kernel, slabs, tiles), grid=(sla...]
    pallas_call x1, Pallas kernels: 52.9 us -> 62.8 us  [middle(): pl.pallas_call(functools.partial(middle_kernel, bits, len(first)), in_spe...]
where the time goes in v5:
time: 68.6 us; the launch traced here: 68.4 us
  Pallas kernels  66.4 us (97%)
  local copies, waits for them, and re-layouts  1.2 us (2%)
  between operations  0.73 us (1%)
    pallas_call x1, Pallas kernels, middle(): pl.pallas_call(functools.partial(middle_kernel, bits, len(first)), in_spe...  62.8 us
    pallas_call x1, Pallas kernels, merge_level(): pl.pallas_call(merge_kernel, out_shape=jax.ShapeDtypeStruct((final, plane...  3.68 us

profile of v5, /device:TPU:0, one launch (start us, length us, event | category | flops | bytes accessed | tf_op | source)
XLA Modules:
  0.0 68.4 jit_solution(9818497281709234785)
XLA Ops:
  0.0 0.0 copy-start.2
  0.0 0.0 copy-start.1
  0.7 62.8 %middle.1.joined = bf16[6,10,64,128]{3,2,1,0:T(8,128)(2,1)} custom-call(bf16[6,4096]{1,0:T(8,128)(2,1)} %feat.1, s32[1,4096]{1,0:T(1,128)} %bitcast.7, s32[1,4096]{1,0:T(1,128)} %bitcast.8, s32[1,4096]{1,0:T(1,128)} %bitcast.9, s32[1]{0:T(128)S(6)} %copy.13.live, bf16[3,3,18,64]{3,2,1,0:T(8,128)(2,1)} %bitcast.6, bf16[3,3,64,192]{3,2,1,0:T(8,128)(2,1)} %rest_1_.1, ...), custom_call_target="tpu_custom_call" | custom-call | tf_op jit(solution)/shard_map/middle/pallas_call | solution.py:488
  63.5 0.0 copy-done.2
  63.5 0.0 copy-done.1
  63.5 0.0 copy-start
  63.5 1.2 %copy-done = bf16[6,10,64,128]{3,2,1,0:T(8,128)(2,1)S(1)} copy-done((bf16[6,10,64,128]{3,2,1,0:T(8,128)(2,1)S(1)}, bf16[6,10,64,128]{3,2,1,0:T(8,128)(2,1)}, u32[]{:S(2)}) %copy-start) | copy-done | bytes 983064
  64.7 3.7 %merge_level.1 = f32[3,4,8,128]{3,2,1,0:T(8,128)} custom-call(bf16[6,10,64,128]{3,2,1,0:T(8,128)(2,1)S(1)} %copy-done, bf16[3,3,64,192]{3,2,1,0:T(8,128)(2,1)S(1)} %copy-done.1, bf16[3,64]{1,0:T(4,128)(2,1)S(1)} %copy-done.2), custom_call_target="tpu_custom_call" | custom-call | tf_op jit(solution)/shard_map/merge_level/pallas_call | solution.py:535
Async XLA Ops:
  0.0 63.5 %copy-start.2 = (bf16[3,64]{1,0:T(4,128)(2,1)S(1)}, bf16[3,64]{1,0:T(4,128)(2,1)}, u32[]{:S(2)}) copy-start(bf16[3,64]{1,0:T(4,128)(2,1)} %head.1) | copy-start | bytes 1156
  0.0 63.5 %copy-start.1 = (bf16[3,3,64,192]{3,2,1,0:T(8,128)(2,1)S(1)}, bf16[3,3,64,192]{3,2,1,0:T(8,128)(2,1)}, u32[]{:S(2)}) copy-start(bf16[3,3,64,192]{3,2,1,0:T(8,128)(2,1)} %weight.1) | copy-start | bytes 663556
  63.5 1.2 %copy-start = (bf16[6,10,64,128]{3,2,1,0:T(8,128)(2,1)S(1)}, bf16[6,10,64,128]{3,2,1,0:T(8,128)(2,1)}, u32[]{:S(2)}) copy-start(bf16[6,10,64,128]{3,2,1,0:T(8,128)(2,1)} %middle.1.joined) | copy-start | bytes 2949124
